TPU v7x, 512 devices: a whole 4x4x16 slice. The times are simulated.
512 devices in a mesh: layer: 8 (over z_hi, y), pos: 64 (over x, z_lo, core).
Axes of the slice: x: 4, y: 4, z: 16 (z_hi: 2, z_lo: 8; z = z_hi * 8 + z_lo), core: 2. Of those that a mesh axis runs over, the one named last changes fastest.
Arguments:
- layer_inputs: bfloat16 [8, 128, 16, 16, 128], P('layer', 'pos'), may hold values from -6 to 6
- output_grads: bfloat16 [8, 128, 16, 16, 128], P('layer', 'pos'), may hold values from -2 to 2
- input_inverse: float32 [8, 1152, 1152], P('layer', 'pos'), may hold values from -0.06 to 2.1
- grad_inverse: float32 [8, 128, 128], P('layer'), may hold values from -4 to 54
Outputs:
- update: float32 [8, 1152, 128], P('layer', 'pos')
- grad_grams: float32 [8, 2, 128, 128], P('layer')
All inputs are finite; a program needn't handle non-finite values.
Results may differ from a plain program's by a relative error of at most 0.0023.
Values may be sent and summed in bfloat16 or wider, within the bound.
A program may use at most 64 MiB of HBM per device.

v0:
```python
import jax
import jax.numpy as jnp
from jax import lax
from jax.sharding import PartitionSpec as P


def shifted(block, axis, distance):
    devices = range(lax.axis_size(axis))
    route = [(i - distance, i) for i in devices if i - distance in devices]
    return lax.ppermute(block, axis, route)


def pad_maps(layer_maps):
    return jnp.pad(layer_maps, ((0, 0), (1, 1), (1, 1), (0, 0)))


def unfold_piece(padded, kernel_tap, width):
    offset_row = kernel_tap // 3
    offset_col = kernel_tap % 3
    side = padded.shape[1] - 2
    return padded[:, offset_row : offset_row + side, offset_col : offset_col + side, :].reshape(
        -1, width
    )


def apply_patches(padded_maps, precond_all, row_count, width):
    mapped = jnp.zeros((row_count, width), jnp.float32)
    for kernel_tap in range(9):
        mapped = mapped + jnp.dot(
            unfold_piece(padded_maps, kernel_tap, width),
            precond_all[kernel_tap * width : (kernel_tap + 1) * width],
            preferred_element_type=jnp.float32,
        )
    return mapped.astype(jnp.bfloat16)


def per_device(layer_inputs, output_grads, input_inverse, grad_inverse):
    high = lax.Precision.HIGHEST
    layer_maps = layer_inputs[0]
    grad_maps = output_grads[0]
    width = layer_maps.shape[3]
    row_count = layer_maps.shape[0] * layer_maps.shape[1] * layer_maps.shape[2]
    scale_all = 1.0 / (row_count * lax.axis_size("pos"))
    maps_after, grads_after = shifted((layer_maps, grad_maps), "layer", -1)
    padded = pad_maps(layer_maps)
    grad_rows = grad_maps.reshape(-1, width)
    blocks = [
        jnp.dot(
            unfold_piece(padded, kernel_tap, width).T, grad_rows, preferred_element_type=jnp.float32
        )
        for kernel_tap in range(9)
    ]
    grad_part = jnp.concatenate(blocks, axis=0)
    own_part = jnp.dot(grad_rows.T, grad_rows, preferred_element_type=jnp.float32)
    cross_part = jnp.dot(
        grad_rows.T, grads_after.reshape(-1, width), preferred_element_type=jnp.float32
    )
    grad_sum, own_sum, cross_sum = lax.psum((grad_part, own_part, cross_part), "pos")
    grad_w = grad_sum * scale_all
    g_own = own_sum * scale_all
    g_cross = cross_sum * scale_all
    inverse_rows = input_inverse[0]
    grad_inv = grad_inverse[0]
    precond_mine = jnp.dot(
        jnp.dot(inverse_rows, grad_w, precision=high), grad_inv, precision=high
    ).astype(jnp.bfloat16)
    padded_after = pad_maps(maps_after)
    precond_layer = lax.all_gather(precond_mine, "pos", axis=0, tiled=True)
    precond_all = shifted(precond_layer, "layer", -1)
    mapped = apply_patches(padded_after, precond_all, row_count, width)
    blocks = [
        jnp.dot(
            unfold_piece(padded, kernel_tap, width).T, mapped, preferred_element_type=jnp.float32
        )
        for kernel_tap in range(9)
    ]
    cross_local = jnp.concatenate(blocks, axis=0)
    cross_term = lax.psum(cross_local, "pos") * scale_all
    corrected = grad_w - jnp.dot(cross_term, g_cross.T, precision=high)
    update = jnp.dot(jnp.dot(inverse_rows, corrected, precision=high), grad_inv, precision=high)
    grad_grams = jnp.stack([g_own, g_cross], axis=0)
    return (update[None], grad_grams[None])


def solution(mesh):
    return jax.shard_map(
        per_device,
        mesh=mesh,
        in_specs=(
            P("layer", "pos", None, None, None),
            P("layer", "pos", None, None, None),
            P("layer", "pos", None),
            P("layer", None, None),
        ),
        out_specs=(P("layer", "pos", None), P("layer", None, None, None)),
        check_vma=False,
    )
```

profile of v0, /device:TPU:25, one launch (start us, length us, event | category | flops | bytes accessed | tf_op | source)
XLA Modules:
  0.0 1768.3 jit_solution(3532406989465179522)
XLA Ops:
  7.2 1.8 pad_slice_fusion.8
  9.3 0.2 convolution_dynamic-update-slice_fusion.14
  9.5 0.2 convolution_dynamic-update-slice_fusion.13
  9.8 0.2 convolution_dynamic-update-slice_fusion.12
  10.0 0.7 copy-done.6
  10.9 0.2 convolution_dynamic-update-slice_fusion.11
  11.4 0.2 convolution_dynamic-update-slice_fusion.9
  11.6 0.2 convolution_dynamic-update-slice_fusion.8
  11.8 0.8 copy-done.4
  12.7 2.4 collective-permute-start
  15.1 2.2 collective-permute-start.2
  17.3 0.9 convolution_bitcast_fusion.1
  18.2 793.9 %all-reduce.6.cloned.1.call-done = f32[1152,128]{1,0:T(8,128)} async-done(((f32[1152,128]{1,0:T(8,128)}), f32[1152,128]{1,0:T(8,128)}) %all-reduce.6.cloned.1.call-update) | async-done | bytes 589840 | tf_op jit(solution)/shard_map/psum | solution.py:58
  812.1 1.5 fusion.12
  813.8 121.5 %all-gather = bf16[64,18,128]{2,1,0:T(8,128)(2,1)S(1)} all-gather(bf16[1,18,128]{2,1,0:T(8,128)(2,1)S(1)} %fusion.10), channel_id=1, replica_groups=mesh['layer'=8,'pos'=64] {'pos'}, dimensions={0}, use_global_device_ids=true | all-gather | bytes 299520 | tf_op jit(solution)/shard_map/all_gather | solution.py:68
  935.5 2.5 collective-permute-start.1
  938.1 0.9 fusion.46
  939.0 17.6 collective-permute-done.1
  957.9 0.2 fusion.7
  958.4 0.2 convolution_dynamic-update-slice_fusion.6
  958.6 0.2 convolution_dynamic-update-slice_fusion.5
  958.9 0.2 convolution_dynamic-update-slice_fusion.4
  959.1 0.2 fusion.8
  959.4 0.2 convolution_dynamic-update-slice_fusion.3
  959.6 0.2 convolution_dynamic-update-slice_fusion.2
  960.3 0.8 copy-done.3
  961.1 795.7 %all-reduce.8.cloned.1.call-done = (f32[1152,128]{1,0:T(8,128)}, f32[128,128]{1,0:T(8,128)}, f32[128,128]{1,0:T(8,128)}) async-done(((f32[1152,128]{1,0:T(8,128)}, f32[128,128]{1,0:T(8,128)}, f32[128,128]{1,0:T(8,128)}), (f32[1152,128]{1,0:T(8,128)}, f32[128,128]{1,0:T(8,128)}, f32[128,128]{1,0:T(8,128)})) %all-reduce.8.cloned.1.call-update) | async-done | bytes 720912 | tf_op jit(solution)/shard_map/psum | solution.py:78
  1756.9 0.9 multiply_bitcast_fusion
  1757.8 1.7 convolution_subtract_fusion
  1759.5 0.5 fusion.16
  1760.2 0.6 copy.11
  1760.8 0.7 maximum_bitcast_fusion
  (37 shorter events, 3.4 us)
Async XLA Ops:
  7.2 806.5 %copy-start = (f32[1,128,128]{2,1,0:T(8,128)S(1)}, f32[1,128,128]{2,1,0:T(8,128)}, u32[]{:S(2)}) copy-start(f32[1,128,128]{2,1,0:T(8,128)} %param.7) | copy-start | bytes 196612
  7.2 804.9 %all-reduce.6.cloned.1.call-start = ((), (), s32[]{:S(2)}) async-start(), calls=%async_computation | async-start | bytes 1179648 | tf_op jit(solution)/shard_map/psum | solution.py:58
  7.2 1.8 copy-start.1
  9.7 0.9 copy-start.6
  11.8 0.8 copy-start.4
  12.7 1744.2 %all-reduce.8.cloned.1.call-start = ((), (), s32[]{:S(2)}) async-start(), calls=%async_computation.1 | async-start | bytes 1441792 | tf_op jit(solution)/shard_map/psum | solution.py:78
  12.7 925.2 %collective-permute-start = (bf16[2,16,16,128]{3,2,1,0:T(8,128)(2,1)S(1)}, bf16[2,16,16,128]{3,2,1,0:T(8,128)(2,1)S(1)}, u32[]{:S(2)}, u32[]{:S(2)}) collective-permute-start(bf16[2,16,16,128]{3,2,1,0:T(8,128)(2,1)S(1)} %bitcast.140), channel_id=1, source_target_pairs={{64,0},{128,64},{192,128},{256,192},{320,256},{384,320},{448,384},... | collective-permute-start | bytes 393224 | tf_op jit(solution)/shard_map/ppermute | solution.py:10
  15.1 797.0 %copy-start.5 = (f32[1,18,1152]{2,0,1:T(1,128)S(1)}, f32[1,18,1152]{2,0,1:T(1,128)}, u32[]{:S(2)}) copy-start(f32[1,18,1152]{2,0,1:T(1,128)} %param.6) | copy-start | bytes 248836
  15.1 923.0 %collective-permute-start.2 = (bf16[2,16,16,128]{3,2,1,0:T(8,128)(2,1)S(1)}, bf16[2,16,16,128]{3,2,1,0:T(8,128)(2,1)S(1)}, u32[]{:S(2)}, u32[]{:S(2)}) collective-permute-start(bf16[2,16,16,128]{3,2,1,0:T(8,128)(2,1)S(1)} %bitcast.120), channel_id=1, source_target_pairs={{64,0},{128,64},{192,128},{256,192},{320,256},{384,320},{448,384},... | collective-permute-start | bytes 393224 | tf_op jit(solution)/shard_map/ppermute | solution.py:10
  935.5 21.1 %collective-permute-start.1 = (bf16[1152,128]{1,0:T(8,128)(2,1)S(1)}, bf16[1152,128]{1,0:T(8,128)(2,1)S(1)}, u32[]{:S(2)}, u32[]{:S(2)}) collective-permute-start(bf16[1152,128]{1,0:T(8,128)(2,1)S(1)} %reshape.98), channel_id=1, source_target_pairs={{64,0},{128,64},{192,128},{256,192},{320,256},{384,320},{448,384},... | collective-permute-start | bytes 884744 | tf_op jit(solution)/shard_map/ppermute | solution.py:10
  960.1 797.7 %copy-start.2 = (f32[1152,128]{1,0:T(8,128)S(1)}, f32[1152,128]{1,0:T(8,128)}, u32[]{:S(2)}) copy-start(f32[1152,128]{1,0:T(8,128)} %all-reduce.6.cloned.1.call-done) | copy-start | bytes 1769476
  960.3 0.8 copy-start.3
  1756.9 0.9 copy-start.7
Sparse Core Ops, SparseCore 0:
  12.8 799.2 all-reduce.5
  961.3 795.5 all-reduce.7
where the time goes:
time: 1770 us
  waiting for transfers between devices  1610 us (91%)
  blocking collectives  122 us (7%)
    psum x1, waiting for transfers between devices, per_device(): cross_term = lax.psum(cross_local, 'pos') * scale_all  796 us
    psum x1, waiting for transfers between devices, per_device(): lax.psum((grad_part, own_part, cross_part), 'pos')  794 us
    all_gather x1, blocking collectives, per_device(): precond_layer = lax.all_gather(precond_mine, 'pos', axis=0, tiled=True)  122 us
  transfers between devices with their start and end apart: 5, of which 3 were waited for; matrix products, arithmetic and copies ran while one was open for 0% of the time, Pallas kernels for 0%

commit v1 on v0

v1 whole, which is shorter than its diff:
```python
import functools

import jax
import jax.numpy as jnp
from jax import lax
from jax.experimental import pallas as pl
from jax.experimental.pallas import tpu as pltpu
from jax.sharding import PartitionSpec as P

NX, NZ, NC = 4, 8, 2
ROOT = 3
TAPS = 9
MESH = pl.DeviceIdType.MESH
F32 = jnp.float32
BF16 = jnp.bfloat16
HIGH = lax.Precision.HIGHEST


def peers():
    order = sorted(range(NX), key=lambda d: -min(d, NX - d))
    return [(dx, dc) for dx in order for dc in range(NC) if dx or dc]


def rcopy(src, dst, send_sem, recv_sem, to):
    return pltpu.make_async_remote_copy(
        src_ref=src,
        dst_ref=dst,
        send_sem=send_sem,
        recv_sem=recv_sem,
        device_id=to,
        device_id_type=MESH,
    )


def dot(a, b, contract=(1, 0), precision=None):
    return lax.dot_general(
        a,
        b,
        (((contract[0],), (contract[1],)), ((), ())),
        precision=precision,
        preferred_element_type=F32,
    )


def unfold(src, dst, images, side, width):
    area = side * side
    rows = images * area
    value = src[...].astype(F32)
    col = lax.rem(lax.broadcasted_iota(jnp.int32, (rows, width), 0), side)
    before = jnp.where(col == 0, 0.0, pltpu.roll(value, 1, 0))
    after = jnp.where(col == side - 1, 0.0, pltpu.roll(value, rows - 1, 0))
    edge = jnp.zeros((side, width), BF16)
    for s, piece in enumerate((before, value, after)):
        piece = piece.astype(BF16)
        for image in range(images):
            top = image * area
            one = piece[top : top + area]
            lanes = pl.ds(s * width, width)
            dst[pl.ds(top, side), lanes] = edge
            dst[pl.ds(top + side, area - side), lanes] = one[: area - side]
            lanes = pl.ds((3 + s) * width, width)
            dst[pl.ds(top, area), lanes] = one
            lanes = pl.ds((6 + s) * width, width)
            dst[pl.ds(top, area - side), lanes] = one[side:]
            dst[pl.ds(top + area - side, side), lanes] = edge


def kernel(
    layers,
    images,
    side,
    scale,
    x_ref,
    g_ref,
    a_ref,
    ginv_ref,
    upd_ref,
    gram_ref,
    patches,
    patches_next,
    grad_t,
    x_next,
    g_next,
    part,
    part_one,
    in_one,
    out_two,
    in_two,
    plane_sum,
    z_out,
    z_in,
    z_out_wide,
    z_in_wide,
    full,
    full_wide,
    a_in,
    a_all,
    a_two,
    pre,
    rows_full,
    base,
    result,
    result_out,
    result_in,
    gram_part,
    gram_in,
    gram_z_out,
    gram_z_in,
    gram_full,
    ex_send,
    ex_recv,
    z_send,
    z_recv,
    a_send,
    a_recv,
    shift_send,
    shift_recv,
    pre_send,
    pre_recv,
    bc_send,
    bc_recv,
    up_send,
    up_recv,
):
    layer = lax.axis_index("layer")
    pos = lax.axis_index("pos")
    c = lax.rem(pos, NC)
    z = lax.rem(lax.div(pos, NC), NZ)
    x = lax.div(pos, NC * NZ)
    me = x * NC + c
    n = NX * NC
    width = g_ref.shape[1]
    lanes = TAPS * width
    per = NZ // NC
    own_rows = a_ref.shape[0]
    is_root = z == ROOT
    is_rim = z != ROOT
    has_next = layer < layers - 1
    has_prev = layer > 0

    def dev(lay, px, pz, pc):
        return (lay, (px * NZ + pz) * NC + pc)

    def peer(dx, dc):
        return lax.rem(x + dx, NX), lax.rem(c + dc, NC)

    def origin(dx, dc):
        return lax.rem(x + NX - dx, NX) * NC + lax.rem(c + NC - dc, NC)

    barrier = pltpu.get_barrier_semaphore()

    def greet(to):
        pl.semaphore_signal(barrier, inc=1, device_id=to, device_id_type=MESH)

    for dx, dc in peers():
        px, pc = peer(dx, dc)
        greet(dev(layer, px, z, pc))

    @pl.when(is_rim)
    def _():
        for pc in range(NC):
            greet(dev(layer, x, ROOT, pc))

    @pl.when(is_root)
    def _():
        for pz in range(NZ):
            if pz != ROOT:
                for pc in range(NC):
                    greet(dev(layer, x, pz, pc))

    @pl.when(has_prev)
    def _():
        greet(dev(layer - 1, x, z, c))

    @pl.when(has_next)
    def _():
        greet(dev(layer + 1, x, z, c))

    @pl.when(has_prev & is_root)
    def _():
        for pz in range(NZ):
            if pz != ROOT:
                greet(dev(layer - 1, x, pz, c))

    @pl.when(has_next & is_rim)
    def _():
        greet(dev(layer + 1, x, ROOT, c))

    unfold(x_ref, patches, images, side, width)
    grad_t[...] = g_ref[...].T

    root = is_root.astype(jnp.int32)
    nxt = has_next.astype(jnp.int32)
    prv = has_prev.astype(jnp.int32)
    expected = n - 1 + prv + nxt
    expected = expected + root * ((NZ - 1) * NC + prv * (NZ - 1))
    expected = expected + (1 - root) * (NC + nxt)
    pl.semaphore_wait(barrier, expected)

    map_shift = rcopy(x_ref, x_next, shift_send.at[0], shift_recv.at[0], dev(layer - 1, x, z, c))
    grad_shift = rcopy(g_ref, g_next, shift_send.at[1], shift_recv.at[1], dev(layer - 1, x, z, c))

    @pl.when(has_prev)
    def _():
        map_shift.start()

    half = lax.div(z, per)
    slot = lax.rem(z, per) * NC + c
    a_self = is_root & (half == c)
    a_other = jnp.logical_not(a_self)
    a_remote = rcopy(a_ref, a_in.at[slot], a_send.at[0], a_recv.at[slot], dev(layer, x, ROOT, half))
    a_local = pltpu.make_async_copy(a_ref, a_in.at[slot], a_recv.at[slot])

    @pl.when(a_other)
    def _():
        a_remote.start()

    @pl.when(a_self)
    def _():
        a_local.start()

    def scatter(kind, src, dst):
        copies = []
        for dx, dc in peers():
            px, pc = peer(dx, dc)
            s = dx * NC + dc
            copy = rcopy(
                src.at[px * NC + pc],
                dst.at[s],
                ex_send.at[kind, s],
                ex_recv.at[kind, s],
                dev(layer, px, z, pc),
            )
            copy.start()
            copies.append(copy)
        return copies

    def gather(kind, buf):
        copies = []
        for dx, dc in peers():
            px, pc = peer(dx, dc)
            s = dx * NC + dc
            copy = rcopy(
                buf.at[me],
                buf.at[me],
                ex_send.at[kind, s],
                ex_recv.at[kind, s],
                dev(layer, px, z, pc),
            )
            copy.start()
            copies.append(copy)
        return copies

    def gathered(kind, buf):
        for dx, dc in reversed(peers()):
            s = dx * NC + dc
            block = buf.at[origin(dx, dc)]
            rcopy(
                block, block, ex_send.at[kind, s], ex_recv.at[kind, s], dev(layer, x, z, c)
            ).wait_recv()

    def sent(copies):
        for copy in copies:
            copy.wait_send()

    def z_copy(kind, src, dst):
        return rcopy(
            src, dst.at[z], z_send.at[kind], z_recv.at[kind, z], dev(layer, x, ROOT, c)
        )

    def z_arrived(kind, src, dst, pz):
        rcopy(
            src, dst.at[pz], z_send.at[kind], z_recv.at[kind, pz], dev(layer, x, ROOT, c)
        ).wait_recv()

    z_bufs = ((z_out_wide, z_in_wide), (z_out, z_in))

    def reduce_plane(kind, product, part, out, inn):
        part[...] = product.reshape(part.shape)
        if out is not part:
            out[...] = product.astype(BF16).reshape(out.shape)
        return scatter(kind, out, inn)

    def finish_plane(copies, part, inn, z_slot):
        total = part[me]
        for copy, (dx, dc) in reversed(list(zip(copies, peers()))):
            copy.wait_recv()
            total = total + inn[dx * NC + dc].astype(F32)
        plane_sum[...] = total

        src, dst = z_bufs[z_slot]

        @pl.when(is_rim)
        def _():
            src[...] = total.astype(src.dtype)
            z_copy(z_slot, src, dst).start()

    def root_total(z_slot, buf):
        total = plane_sum[...]
        src, dst = z_bufs[z_slot]
        for pz in range(NZ):
            if pz != ROOT:
                z_arrived(z_slot, src, dst, pz)
                total = total + dst[pz].astype(F32)
        buf[me] = (total * scale).astype(buf.dtype)

    def fold(both):
        half_rows = both.shape[0] // 2
        return both[:half_rows] + both[half_rows:]

    def times_inverse(buf):
        value = buf[...].reshape(width, lanes)
        top = value.astype(BF16)
        low = (value - top.astype(F32)).astype(BF16)
        both = dot(a_two[...], jnp.concatenate([top, low], axis=0), (1, 1))
        return fold(both[:, :width] + both[:, width:])

    first = reduce_plane(0, dot(grad_t[...], patches[...]), part_one, part_one, in_one)
    finish_plane(first, part_one, in_one, 0)

    @pl.when(has_prev)
    def _():
        grad_shift.start()

    pre_copies = [
        rcopy(
            rows_full,
            pre.at[me],
            pre_send.at[pz],
            pre_recv.at[0],
            dev(layer - 1, x, pz, c),
        )
        for pz in range(NZ)
    ]

    @pl.when(is_root)
    def _():
        for q in range(NZ):
            pltpu.make_async_copy(a_ref, a_in.at[q], a_recv.at[q]).wait()
            a_all[pl.ds(q * own_rows, own_rows), :] = a_in[q]
        rows = a_all[...]
        top = rows.astype(BF16)
        a_two[pl.ds(0, rows.shape[0]), :] = top
        a_two[pl.ds(rows.shape[0], rows.shape[0]), :] = (rows - top.astype(F32)).astype(BF16)
        root_total(0, full_wide)
        copies = gather(1, full_wide)
        gathered(1, full_wide)
        value = dot(times_inverse(full_wide), ginv_ref[...], precision=HIGH)
        base[...] = value
        rows_full[...] = value.astype(BF16)

        @pl.when(has_prev)
        def _():
            for copy in pre_copies:
                copy.start()

        sent(copies)

    @pl.when(has_next)
    def _():
        map_shift.wait_recv()

    @pl.when(jnp.logical_not(has_next))
    def _():
        x_next[...] = jnp.zeros_like(x_next)
        g_next[...] = jnp.zeros_like(g_next)
        pre[...] = jnp.zeros_like(pre)

    unfold(x_next, patches_next, images, side, width)

    @pl.when(has_next)
    def _():
        grad_shift.wait_recv()

    blocks = gram_part.shape[0] // 2
    gram_part[pl.ds(0, blocks)] = dot(grad_t[...], g_ref[...]).reshape(
        blocks, gram_part.shape[1], width
    )
    gram_part[pl.ds(blocks, blocks)] = dot(grad_t[...], g_next[...]).reshape(
        blocks, gram_part.shape[1], width
    )
    gram_copies = scatter(2, gram_part, gram_in)

    @pl.when(has_next)
    def _():
        rcopy(
            rows_full, pre.at[me], pre_send.at[0], pre_recv.at[0], dev(layer, x, z, c)
        ).wait_recv()
        copies = gather(3, pre)
        gathered(3, pre)
        sent(copies)

    mapped = dot(patches_next[...], pre[...].reshape(lanes, width)).astype(BF16)
    second = reduce_plane(4, dot(mapped.T, patches[...]), part, out_two, in_two)

    gram = gram_part[me]
    for copy, (dx, dc) in reversed(list(zip(gram_copies, peers()))):
        copy.wait_recv()
        gram = gram + gram_in[dx * NC + dc]
    gram_z_out[...] = gram

    @pl.when(is_rim)
    def _():
        z_copy(2, gram_z_out, gram_z_in).start()

    finish_plane(second, part, in_two, 1)

    bc_copies = [
        rcopy(
            gram_full.at[me],
            gram_full.at[me],
            bc_send.at[pz],
            bc_recv.at[0],
            dev(layer, x, pz, c),
        )
        for pz in range(NZ)
    ]

    @pl.when(is_root)
    def _():
        total = gram_z_out[...]
        for pz in range(NZ):
            if pz != ROOT:
                z_arrived(2, gram_z_out, gram_z_in, pz)
                total = total + gram_z_in[pz]
        gram_full[me] = total * scale
        for pz in range(NZ):
            if pz != ROOT:
                bc_copies[pz].start()

    @pl.when(is_rim)
    def _():
        bc_copies[ROOT].wait_recv()

    gram_gather = gather(5, gram_full)

    @pl.when(is_root)
    def _():
        root_total(1, full)
        copies = gather(6, full)
        gathered(5, gram_full)
        cross_gram = gram_full[pl.ds(blocks, blocks)].reshape(width, width)
        mix = dot(cross_gram, ginv_ref[...], (0, 0), HIGH)
        gathered(6, full)
        value = base[...] - dot(times_inverse(full), mix, precision=HIGH)
        result[...] = value
        for q in range(NZ):
            result_out[q] = result[pl.ds(q * own_rows, own_rows), :]
            copy = rcopy(
                result_out.at[q],
                result_in,
                up_send.at[q],
                up_recv.at[0],
                dev(layer, x, c * per + q // NC, q % NC),
            )
            if q // NC == ROOT % per and q % NC == ROOT // per:

                @pl.when(c == ROOT // per)
                def _(q=q):
                    upd_ref[...] = result_out[q]

                @pl.when(c != ROOT // per)
                def _(copy=copy):
                    copy.start()
                    copy.wait_send()
            else:
                copy.start()
        for q in range(NZ):
            if not (q // NC == ROOT % per and q % NC == ROOT // per):
                rcopy(
                    result_out.at[q],
                    result_in,
                    up_send.at[q],
                    up_recv.at[0],
                    dev(layer, x, c * per + q // NC, q % NC),
                ).wait_send()
        sent(copies)

    @pl.when(is_rim)
    def _():
        gathered(5, gram_full)

    gram_ref[...] = gram_full[...].reshape(gram_ref.shape)

    @pl.when(a_other)
    def _():
        rcopy(
            result_out.at[0], result_in, up_send.at[0], up_recv.at[0], dev(layer, x, z, c)
        ).wait_recv()
        upd_ref[...] = result_in[...]

    sent(first)
    sent(second)
    sent(gram_copies)
    sent(gram_gather)

    @pl.when(a_other)
    def _():
        a_remote.wait_send()

    @pl.when(has_prev)
    def _():
        map_shift.wait_send()
        grad_shift.wait_send()

    @pl.when(is_rim)
    def _():
        z_copy(0, z_out_wide, z_in_wide).wait_send()
        z_copy(1, z_out, z_in).wait_send()
        z_copy(2, gram_z_out, gram_z_in).wait_send()

    @pl.when(is_root)
    def _():
        for pz in range(NZ):
            if pz != ROOT:
                bc_copies[pz].wait_send()

    @pl.when(is_root & has_prev)
    def _():
        for copy in pre_copies:
            copy.wait_send()


def per_device(layers, layer_inputs, output_grads, input_inverse, grad_inverse):
    _, images, side, _, width = layer_inputs.shape
    rows = images * side * side
    own_rows = input_inverse.shape[1]
    lanes = TAPS * width
    n = NX * NC
    strip = width // n
    block_rows = lanes // n
    gram_rows = 2 * width // n
    scale = 1.0 / (rows * n * NZ)
    vmem = pltpu.VMEM
    dma = pltpu.SemaphoreType.DMA
    scratch = [
        vmem((rows, lanes), BF16),
        vmem((rows, lanes), BF16),
        vmem((width, rows), BF16),
        vmem((rows, width), BF16),
        vmem((rows, width), BF16),
        vmem((n, strip, lanes), F32),
        vmem((n, strip, lanes), F32),
        vmem((n, strip, lanes), F32),
        vmem((n, strip, lanes), BF16),
        vmem((n, strip, lanes), BF16),
        vmem((strip, lanes), F32),
        vmem((strip, lanes), BF16),
        vmem((NZ, strip, lanes), BF16),
        vmem((strip, lanes), F32),
        vmem((NZ, strip, lanes), F32),
        vmem((n, strip, lanes), F32),
        vmem((n, strip, lanes), F32),
        vmem((NZ, own_rows, lanes), F32),
        vmem((block_rows, lanes), F32),
        vmem((2 * block_rows, lanes), BF16),
        vmem((n, block_rows, width), BF16),
        vmem((block_rows, width), BF16),
        vmem((block_rows, width), F32),
        vmem((block_rows, width), F32),
        vmem((NZ, own_rows, width), F32),
        vmem((own_rows, width), F32),
        vmem((n, gram_rows, width), F32),
        vmem((n, gram_rows, width), F32),
        vmem((gram_rows, width), F32),
        vmem((NZ, gram_rows, width), F32),
        vmem((n, gram_rows, width), F32),
        dma((7, n)),
        dma((7, n)),
        dma((3,)),
        dma((3, NZ)),
        dma((1,)),
        dma((NZ,)),
        dma((2,)),
        dma((2,)),
        dma((NZ,)),
        dma((1,)),
        dma((NZ,)),
        dma((1,)),
        dma((NZ,)),
        dma((1,)),
    ]
    whole = pl.BlockSpec(memory_space=pltpu.VMEM)
    update, grams = pl.pallas_call(
        functools.partial(kernel, layers, images, side, scale),
        out_shape=(
            jax.ShapeDtypeStruct((own_rows, width), F32),
            jax.ShapeDtypeStruct((2, width, width), F32),
        ),
        in_specs=[whole] * 4,
        out_specs=(whole, whole),
        scratch_shapes=scratch,
        compiler_params=pltpu.CompilerParams(
            collective_id=0, has_side_effects=True, vmem_limit_bytes=48 * 1024 * 1024
        ),
        name="kfac_step",
    )(
        layer_inputs.reshape(rows, width),
        output_grads.reshape(rows, width),
        input_inverse.reshape(own_rows, lanes),
        grad_inverse.reshape(width, width),
    )
    return update[None], grams[None]


def solution(mesh):
    assert mesh.shape["pos"] == NX * NZ * NC
    return jax.shard_map(
        functools.partial(per_device, mesh.shape["layer"]),
        mesh=mesh,
        in_specs=(
            P("layer", "pos", None, None, None),
            P("layer", "pos", None, None, None),
            P("layer", "pos", None),
            P("layer", None, None),
        ),
        out_specs=(P("layer", "pos", None), P("layer", None, None, None)),
        check_vma=False,
    )
```

time: 1770 us -> 93.3 us (0.05)
  waiting for transfers between devices: 1610 us -> 0 us
  blocking collectives: 122 us -> 0 us
  Pallas kernels: 0 us -> 89.3 us
    psum x2 -> x0, waiting for transfers between devices: 1590 us -> none  [the longest x1 796 us: per_device(): cross_term = lax.psum(cross_local, 'pos') * scale_all]
    all_gather x1 -> x0, blocking collectives: 122 us -> none  [per_device(): precond_layer = lax.all_gather(precond_mine, 'pos', axis=0, tiled=True)]
    pallas_call x0 -> x1, Pallas kernels: none -> 89.3 us  [per_device(): pl.pallas_call(functools.partial(kernel, layers, images, side, scale), ou...]
  transfers between devices with their start and end apart: 5 -> 0, of which waited for: 3 -> 0; matrix products, arithmetic and copies ran while one was open for 0% -> 0% of each run, Pallas kernels for 0% -> 0%
where the time goes in v1:
time: 93.3 us; the launch traced here: 93.1 us
  Pallas kernels  89.3 us (96%)
  local copies, waits for them, and re-layouts  3.11 us (3%)
    pallas_call x1, Pallas kernels, per_device(): pl.pallas_call(functools.partial(kernel, layers, images, side, scale), ou...  89.3 us
    unnamed x9, local copies, waits for them, and re-layouts  3.11 us

profile of v1, /device:TPU:25, one launch (start us, length us, event | category | flops | bytes accessed | tf_op | source)
XLA Modules:
  0.0 93.1 jit_solution(750903408687261284)
XLA Ops:
  0.6 0.0 copy-start
  0.6 0.0 copy-start.2
  0.6 0.9 %copy.9 = f32[1,18,1152]{2,1,0:T(8,128)S(1)} copy(f32[1,18,1152]{2,0,1:T(1,128)} %param.6) | data formatting | bytes 165888
  1.6 0.0 copy-done
  1.6 0.0 copy-done.2
  1.6 0.0 copy-start.1
  1.6 0.9 copy-done.1
  2.5 89.3 %kfac_step.1 = (f32[18,128]{1,0:T(8,128)S(1)}, f32[2,128,128]{2,1,0:T(8,128)S(1)}) custom-call(bf16[512,128]{1,0:T(8,128)(2,1)S(1)} %bitcast.9, bf16[512,128]{1,0:T(8,128)(2,1)S(1)} %bitcast.10, f32[18,1152]{1,0:T(8,128)S(1)} %bitcast.8, f32[128,128]{1,0:T(8,128)S(1)} %bitcast.12), custom_call_target="tpu_custom_call" | custom-call | tf_op jit(solution)/shard_map/kfac_step/pallas_call | solution.py:584
  91.9 0.6 copy.6
  92.5 0.7 copy.11
Async XLA Ops:
  0.6 1.0 %copy-start = (bf16[1,2,16,16,128]{4,3,2,1,0:T(8,128)(2,1)S(1)}, bf16[1,2,16,16,128]{4,3,2,1,0:T(8,128)(2,1)}, u32[]{:S(2)}) copy-start(bf16[1,2,16,16,128]{4,3,2,1,0:T(8,128)(2,1)} %param.4) | copy-start | bytes 393220
  0.6 1.0 %copy-start.2 = (f32[1,128,128]{2,1,0:T(8,128)S(1)}, f32[1,128,128]{2,1,0:T(8,128)}, u32[]{:S(2)}) copy-start(f32[1,128,128]{2,1,0:T(8,128)} %param.7) | copy-start | bytes 196612
  1.6 0.9 copy-start.1

commit v2 on v1

v2 whole, which is shorter than its diff:
```python
import functools

import jax
import jax.numpy as jnp
from jax import lax
from jax.experimental import pallas as pl
from jax.experimental.pallas import tpu as pltpu
from jax.sharding import PartitionSpec as P

NX, NY, NZ, NC = 4, 4, 8, 2
ROOT = 3
TAPS = 9
MESH = pl.DeviceIdType.MESH
F32 = jnp.float32
BF16 = jnp.bfloat16
HIGH = lax.Precision.HIGHEST


def offsets():
    return sorted(range(1, NX), key=lambda d: -min(d, NX - d))


def rcopy(src, dst, send_sem, recv_sem, to):
    return pltpu.make_async_remote_copy(
        src_ref=src,
        dst_ref=dst,
        send_sem=send_sem,
        recv_sem=recv_sem,
        device_id=to,
        device_id_type=MESH,
    )


def dot(a, b, contract=(1, 0), precision=None):
    return lax.dot_general(
        a,
        b,
        (((contract[0],), (contract[1],)), ((), ())),
        precision=precision,
        preferred_element_type=F32,
    )


def unfold(src, dst, images, side, width):
    area = side * side
    rows = images * area
    value = src[...].astype(F32)
    col = lax.rem(lax.broadcasted_iota(jnp.int32, (rows, width), 0), side)
    before = jnp.where(col == 0, 0.0, pltpu.roll(value, 1, 0))
    after = jnp.where(col == side - 1, 0.0, pltpu.roll(value, rows - 1, 0))
    edge = jnp.zeros((side, width), BF16)
    for s, piece in enumerate((before, value, after)):
        piece = piece.astype(BF16)
        for image in range(images):
            top = image * area
            one = piece[top : top + area]
            lanes = pl.ds(s * width, width)
            dst[pl.ds(top, side), lanes] = edge
            dst[pl.ds(top + side, area - side), lanes] = one[: area - side]
            lanes = pl.ds((3 + s) * width, width)
            dst[pl.ds(top, area), lanes] = one
            lanes = pl.ds((6 + s) * width, width)
            dst[pl.ds(top, area - side), lanes] = one[side:]
            dst[pl.ds(top + area - side, side), lanes] = edge


def kernel(
    layers,
    images,
    side,
    scale,
    x_hbm,
    g_hbm,
    a_ref,
    ginv_hbm,
    upd_ref,
    gram_ref,
    xg_ref,
    ginv_ref,
    patches,
    patches_next,
    grad_t,
    xg_next,
    relay,
    part,
    part_one,
    in_one,
    out_x_one,
    in_x_one,
    out_two,
    in_two,
    out_x_two,
    in_x_two,
    plane_sum,
    z_out,
    z_in,
    z_out_wide,
    z_in_wide,
    full,
    full_wide,
    a_in,
    a_all,
    a_two,
    pre,
    rows_full,
    base,
    result,
    result_out,
    result_in,
    gram_part,
    gram_in,
    gram_out_x,
    gram_in_x,
    gram_z_out,
    gram_z_in,
    gram_full,
    ex_send,
    ex_recv,
    z_send,
    z_recv,
    a_send,
    a_recv,
    shift_send,
    shift_recv,
    relay_send,
    relay_recv,
    far_send,
    far_recv,
    pre_send,
    pre_recv,
    bc_send,
    bc_recv,
    up_send,
    up_recv,
    load_sem,
):
    layer = lax.axis_index("layer")
    pos = lax.axis_index("pos")
    c = lax.rem(pos, NC)
    z = lax.rem(lax.div(pos, NC), NZ)
    x = lax.div(pos, NC * NZ)
    block = x * NC + c
    strip = c * NX + x
    n = NX * NC
    _, rows, width = xg_ref.shape
    quarter = rows // NY
    y = lax.rem(layer, NY)
    lanes = TAPS * width
    per = NZ // NC
    own_rows = result_in.shape[0]
    is_root = z == ROOT
    is_rim = z != ROOT
    has_next = layer < layers - 1
    has_prev = layer > 0
    sends_far = has_prev & (y == 0)
    sends_near = has_prev & (y != 0)
    relays = (layer >= NY) & (y != 0)
    late = has_next & (y == NY - 1)

    def dev(lay, px, pz, pc):
        return (lay, (px * NZ + pz) * NC + pc)

    def ahead(dx):
        return lax.rem(x + dx, NX)

    def behind(dx):
        return lax.rem(x + NX - dx, NX)

    other = NC - 1 - c

    loads = [
        pltpu.make_async_copy(src, dst, load_sem.at[i])
        for i, (src, dst) in enumerate(((x_hbm, xg_ref.at[0]), (g_hbm, xg_ref.at[1]), (ginv_hbm, ginv_ref)))
    ]
    for load in loads:
        load.start()

    barrier = pltpu.get_barrier_semaphore()

    def greet(to):
        pl.semaphore_signal(barrier, inc=1, device_id=to, device_id_type=MESH)

    greet(dev(layer, x, z, other))
    for dx in offsets():
        greet(dev(layer, ahead(dx), z, c))

    @pl.when(is_rim)
    def _():
        for pc in range(NC):
            greet(dev(layer, x, ROOT, pc))

    @pl.when(is_root)
    def _():
        for pz in range(NZ):
            if pz != ROOT:
                for pc in range(NC):
                    greet(dev(layer, x, pz, pc))

    @pl.when(has_next)
    def _():
        greet(dev(layer + 1, x, z, c))

    @pl.when(has_next & is_rim)
    def _():
        greet(dev(layer + 1, x, ROOT, c))

    @pl.when(relays)
    def _():
        greet(dev(layer - y, x, z, c))

    @pl.when(late)
    def _():
        for q in range(1, NY):
            greet(dev(layer + 1 + q, x, z, c))

    for load in loads:
        load.wait()
    unfold(xg_ref.at[0], patches, images, side, width)
    grad_t[...] = xg_ref[1].T

    root = is_root.astype(jnp.int32)
    prv = has_prev.astype(jnp.int32)
    expected = NX + prv + sends_far.astype(jnp.int32) * (NY - 1) + relays.astype(jnp.int32)
    expected = expected + root * ((NZ - 1) * NC + prv * (NZ - 1)) + (1 - root) * NC
    pl.semaphore_wait(barrier, expected)

    shift = rcopy(xg_ref, xg_next, shift_send.at[0], shift_recv.at[0], dev(layer - 1, x, z, c))

    def piece(ref, q):
        return ref.at[:, pl.ds(pl.multiple_of(q * quarter, quarter), quarter)]

    to_relay = [
        rcopy(
            piece(xg_ref, q),
            relay,
            relay_send.at[q],
            relay_recv.at[0],
            dev(layer + q, x, z, c),
        )
        for q in range(1, NY)
    ]
    far_own = rcopy(
        piece(xg_ref, 0), piece(xg_next, 0), far_send.at[0], far_recv.at[0], dev(layer - 1, x, z, c)
    )
    far_relay = rcopy(
        relay, piece(xg_next, y), far_send.at[0], far_recv.at[y], dev(layer - y - 1, x, z, c)
    )

    def arrived():
        @pl.when(has_next & jnp.logical_not(late))
        def _():
            shift.wait_recv()

        @pl.when(late)
        def _():
            for q in range(NY):
                rcopy(
                    relay, piece(xg_next, q), far_send.at[0], far_recv.at[q], dev(layer, x, z, other)
                ).wait_recv()

    half = lax.div(z, per)
    slot = lax.rem(z, per) * NC + c
    a_self = is_root & (half == c)
    a_other = jnp.logical_not(a_self)
    a_remote = rcopy(a_ref, a_in.at[slot], a_send.at[0], a_recv.at[slot], dev(layer, x, ROOT, half))
    a_local = pltpu.make_async_copy(a_ref, a_in.at[slot], a_recv.at[slot])

    @pl.when(a_other)
    def _():
        a_remote.start()

    @pl.when(a_self)
    def _():
        a_local.start()

    @pl.when(sends_near)
    def _():
        shift.start()

    @pl.when(sends_far)
    def _():
        for copy in to_relay:
            copy.start()

    def sent(copies):
        for copy in copies:
            copy.wait_send()

    def plane_start(kind, out, in_core):
        copies = []
        for dx in offsets() + [0]:
            copy = rcopy(
                out.at[other * NX + ahead(dx)],
                in_core.at[dx],
                ex_send.at[kind, dx],
                ex_recv.at[kind, dx],
                dev(layer, x, z, other),
            )
            copy.start()
            copies.append(copy)
        return copies

    def plane_finish(kind, core_copies, part, in_core, out_x, in_x):
        copies = []
        for dx, arrival in zip(offsets(), core_copies):
            arrival.wait_recv()
            out_x[dx] = (part[c * NX + ahead(dx)] + in_core[dx].astype(F32)).astype(out_x.dtype)
            copy = rcopy(
                out_x.at[dx],
                in_x.at[dx],
                ex_send.at[kind, NX + dx],
                ex_recv.at[kind, NX + dx],
                dev(layer, ahead(dx), z, c),
            )
            copy.start()
            copies.append(copy)
        core_copies[-1].wait_recv()
        total = part[strip] + in_core[0].astype(F32)
        for dx, copy in reversed(list(zip(offsets(), copies))):
            copy.wait_recv()
            total = total + in_x[dx].astype(F32)
        return total, copies

    def gather(kind, buf, own):
        copies = []
        for dx in offsets():
            copies.append(
                rcopy(
                    buf.at[own],
                    buf.at[own],
                    ex_send.at[kind, dx],
                    ex_recv.at[kind, dx],
                    dev(layer, ahead(dx), z, c),
                )
            )
        copies.append(
            rcopy(
                buf.at[own],
                buf.at[own],
                ex_send.at[kind, 0],
                ex_recv.at[kind, 0],
                dev(layer, x, z, other),
            )
        )
        return copies

    def gathered(kind, buf, place):
        copies = []
        for dx in reversed(offsets()):
            got = buf.at[place(behind(dx), c)]
            rcopy(
                got, got, ex_send.at[kind, dx], ex_recv.at[kind, dx], dev(layer, x, z, other)
            ).wait_recv()
            copy = rcopy(
                got,
                got,
                ex_send.at[kind, NX + dx],
                ex_recv.at[kind, NX + dx],
                dev(layer, x, z, other),
            )
            copy.start()
            copies.append(copy)
        for slot_of, dx in [(0, 0)] + [(NX + dx, dx) for dx in reversed(offsets())]:
            got = buf.at[place(behind(dx), other)]
            rcopy(
                got,
                got,
                ex_send.at[kind, slot_of],
                ex_recv.at[kind, slot_of],
                dev(layer, x, z, other),
            ).wait_recv()
        return copies

    def by_strip(px, pc):
        return pc * NX + px

    def by_block(px, pc):
        return px * NC + pc

    def z_copy(kind, src, dst):
        return rcopy(
            src, dst.at[z], z_send.at[kind], z_recv.at[kind, z], dev(layer, x, ROOT, c)
        )

    def z_arrived(kind, src, dst, pz):
        rcopy(
            src, dst.at[pz], z_send.at[kind], z_recv.at[kind, pz], dev(layer, x, ROOT, c)
        ).wait_recv()

    z_bufs = ((z_out_wide, z_in_wide), (z_out, z_in))

    def z_start(z_slot, total):
        plane_sum[...] = total
        src, dst = z_bufs[z_slot]

        @pl.when(is_rim)
        def _():
            src[...] = total.astype(src.dtype)
            z_copy(z_slot, src, dst).start()

    def root_total(z_slot, buf):
        total = plane_sum[...]
        src, dst = z_bufs[z_slot]
        for pz in range(NZ):
            if pz != ROOT:
                z_arrived(z_slot, src, dst, pz)
                total = total + dst[pz].astype(F32)
        buf[strip] = total * scale

    def fold(both):
        half_rows = both.shape[0] // 2
        return both[:half_rows] + both[half_rows:]

    def times_inverse(buf):
        value = buf[...].reshape(width, lanes)
        top = value.astype(BF16)
        low = (value - top.astype(F32)).astype(BF16)
        both = dot(a_two[...], jnp.concatenate([top, low], axis=0), (1, 1))
        return fold(both[:, :width] + both[:, width:])

    part_one[...] = dot(grad_t[...], patches[...]).reshape(part_one.shape)
    first = plane_start(0, part_one, in_one)
    total, first_x = plane_finish(0, first, part_one, in_one, out_x_one, in_x_one)
    z_start(0, total)

    @pl.when(jnp.logical_not(has_next))
    def _():
        xg_next[...] = jnp.zeros_like(xg_next)
        pre[...] = jnp.zeros_like(pre)

    half_blocks = gram_part.shape[0] // 2

    def grams():
        arrived()
        shape = (half_blocks, gram_part.shape[1], width)
        gram_part[pl.ds(0, half_blocks)] = dot(grad_t[...], xg_ref[1]).reshape(shape)
        gram_part[pl.ds(half_blocks, half_blocks)] = dot(grad_t[...], xg_next[1]).reshape(shape)
        copies = plane_start(2, gram_part, gram_in)
        gram, copies_x = plane_finish(2, copies, gram_part, gram_in, gram_out_x, gram_in_x)
        gram_z_out[...] = gram

        @pl.when(is_rim)
        def _():
            z_copy(2, gram_z_out, gram_z_in).start()

        sent(copies)
        sent(copies_x)

    @pl.when(jnp.logical_not(late))
    def _():
        grams()

    @pl.when(sends_far)
    def _():
        far_own.start()

    @pl.when(relays)
    def _():
        to_relay[0].wait_recv()
        far_relay.start()

    pre_copies = [
        rcopy(
            rows_full,
            pre.at[block],
            pre_send.at[pz],
            pre_recv.at[0],
            dev(layer - 1, x, pz, c),
        )
        for pz in range(NZ)
    ]

    @pl.when(is_root)
    def _():
        for q in range(NZ):
            pltpu.make_async_copy(a_ref, a_in.at[q], a_recv.at[q]).wait()
            a_all[pl.ds(q * own_rows, own_rows), :] = a_in[q, :, 0, :]
        rows = a_all[...]
        top = rows.astype(BF16)
        a_two[pl.ds(0, rows.shape[0]), :] = top
        a_two[pl.ds(rows.shape[0], rows.shape[0]), :] = (rows - top.astype(F32)).astype(BF16)
        root_total(0, full_wide)
        copies = gather(1, full_wide, strip)
        for copy in copies:
            copy.start()
        passed = gathered(1, full_wide, by_strip)
        value = dot(times_inverse(full_wide), ginv_ref[...], precision=HIGH)
        base[...] = value
        rows_full[...] = value.astype(BF16)

        @pl.when(has_prev)
        def _():
            for copy in pre_copies:
                copy.start()

        sent(copies)
        sent(passed)

    @pl.when(late)
    def _():
        grams()

    unfold(xg_next.at[0], patches_next, images, side, width)

    @pl.when(has_next)
    def _():
        rcopy(
            rows_full, pre.at[block], pre_send.at[0], pre_recv.at[0], dev(layer, x, z, other)
        ).wait_recv()
        copies = gather(3, pre, block)
        for copy in copies:
            copy.start()
        passed = gathered(3, pre, by_block)
        sent(copies)
        sent(passed)

    mapped = dot(patches_next[...], pre[...].reshape(lanes, width)).astype(BF16)
    product = dot(mapped.T, patches[...])
    part[...] = product.reshape(part.shape)
    out_two[...] = product.astype(BF16).reshape(out_two.shape)
    second = plane_start(4, out_two, in_two)
    total, second_x = plane_finish(4, second, part, in_two, out_x_two, in_x_two)
    z_start(1, total)

    bc_copies = [
        rcopy(
            gram_full.at[strip],
            gram_full.at[strip],
            bc_send.at[pz],
            bc_recv.at[0],
            dev(layer, x, pz, c),
        )
        for pz in range(NZ)
    ]

    gram_gather = gather(5, gram_full, strip)

    @pl.when(is_rim)
    def _():
        bc_copies[ROOT].wait_recv()
        for copy in gram_gather:
            copy.start()

    @pl.when(is_root)
    def _():
        root_total(1, full)
        copies = gather(6, full, strip)
        for copy in copies:
            copy.start()
        total = gram_z_out[...]
        for pz in range(NZ):
            if pz != ROOT:
                z_arrived(2, gram_z_out, gram_z_in, pz)
                total = total + gram_z_in[pz]
        gram_full[strip] = total * scale
        for pz in range(NZ):
            if pz != ROOT:
                bc_copies[pz].start()
        for copy in gram_gather:
            copy.start()
        passed = gathered(6, full, by_strip)
        gram_passed = gathered(5, gram_full, by_strip)
        cross_gram = gram_full[pl.ds(half_blocks, half_blocks)].reshape(width, width)
        mix = dot(cross_gram, ginv_ref[...], (0, 0), HIGH)
        value = base[...] - dot(times_inverse(full), mix, precision=HIGH)
        result[...] = value
        for q in range(NZ):
            result_out[q] = result[pl.ds(q * own_rows, own_rows), :]
            copy = rcopy(
                result_out.at[q],
                result_in,
                up_send.at[q],
                up_recv.at[0],
                dev(layer, x, c * per + q // NC, q % NC),
            )
            if q // NC == ROOT % per and q % NC == ROOT // per:

                @pl.when(c == ROOT // per)
                def _(q=q):
                    upd_ref[...] = result_out[q]

                @pl.when(c != ROOT // per)
                def _(copy=copy):
                    copy.start()
                    copy.wait_send()
            else:
                copy.start()
        for q in range(NZ):
            if not (q // NC == ROOT % per and q % NC == ROOT // per):
                rcopy(
                    result_out.at[q],
                    result_in,
                    up_send.at[q],
                    up_recv.at[0],
                    dev(layer, x, c * per + q // NC, q % NC),
                ).wait_send()
        sent(copies)
        sent(passed)
        sent(gram_passed)

    @pl.when(is_rim)
    def _():
        sent(gathered(5, gram_full, by_strip))

    gram_ref[...] = gram_full[...].reshape(gram_ref.shape)

    @pl.when(a_other)
    def _():
        rcopy(
            result_out.at[0], result_in, up_send.at[0], up_recv.at[0], dev(layer, x, z, other)
        ).wait_recv()
        upd_ref[...] = result_in[...]

    sent(first)
    sent(first_x)
    sent(second)
    sent(second_x)
    sent(gram_gather)

    @pl.when(a_other)
    def _():
        a_remote.wait_send()

    @pl.when(sends_near)
    def _():
        shift.wait_send()

    @pl.when(sends_far)
    def _():
        for copy in to_relay:
            copy.wait_send()
        far_own.wait_send()

    @pl.when(relays)
    def _():
        far_relay.wait_send()

    @pl.when(is_rim)
    def _():
        z_copy(0, z_out_wide, z_in_wide).wait_send()
        z_copy(1, z_out, z_in).wait_send()
        z_copy(2, gram_z_out, gram_z_in).wait_send()

    @pl.when(is_root)
    def _():
        for pz in range(NZ):
            if pz != ROOT:
                bc_copies[pz].wait_send()

    @pl.when(is_root & has_prev)
    def _():
        for copy in pre_copies:
            copy.wait_send()


def per_device(layers, layer_inputs, output_grads, input_inverse, grad_inverse):
    _, images, side, _, width = layer_inputs.shape
    rows = images * side * side
    own_rows = input_inverse.shape[1]
    lanes = TAPS * width
    n = NX * NC
    strip = width // n
    block_rows = lanes // n
    gram_rows = 2 * width // n
    scale = 1.0 / (rows * n * NZ)
    vmem = pltpu.VMEM
    dma = pltpu.SemaphoreType.DMA
    scratch = [
        vmem((2, rows, width), BF16),
        vmem((width, width), F32),
        vmem((rows, lanes), BF16),
        vmem((rows, lanes), BF16),
        vmem((width, rows), BF16),
        vmem((2, rows, width), BF16),
        vmem((2, rows // NY, width), BF16),
        vmem((n, strip, lanes), F32),
        vmem((n, strip, lanes), F32),
        vmem((NX, strip, lanes), F32),
        vmem((NX, strip, lanes), F32),
        vmem((NX, strip, lanes), F32),
        vmem((n, strip, lanes), BF16),
        vmem((NX, strip, lanes), BF16),
        vmem((NX, strip, lanes), BF16),
        vmem((NX, strip, lanes), BF16),
        vmem((strip, lanes), F32),
        vmem((strip, lanes), BF16),
        vmem((NZ, strip, lanes), BF16),
        vmem((strip, lanes), F32),
        vmem((NZ, strip, lanes), F32),
        vmem((n, strip, lanes), F32),
        vmem((n, strip, lanes), F32),
        vmem((NZ, own_rows, 1, lanes), F32),
        vmem((block_rows, lanes), F32),
        vmem((2 * block_rows, lanes), BF16),
        vmem((n, block_rows, width), BF16),
        vmem((block_rows, width), BF16),
        vmem((block_rows, width), F32),
        vmem((block_rows, width), F32),
        vmem((NZ, own_rows, width), F32),
        vmem((own_rows, width), F32),
        vmem((n, gram_rows, width), F32),
        vmem((NX, gram_rows, width), F32),
        vmem((NX, gram_rows, width), F32),
        vmem((NX, gram_rows, width), F32),
        vmem((gram_rows, width), F32),
        vmem((NZ, gram_rows, width), F32),
        vmem((n, gram_rows, width), F32),
        dma((7, n)),
        dma((7, n)),
        dma((3,)),
        dma((3, NZ)),
        dma((1,)),
        dma((NZ,)),
        dma((1,)),
        dma((1,)),
        dma((NY,)),
        dma((1,)),
        dma((NY,)),
        dma((NY,)),
        dma((NZ,)),
        dma((1,)),
        dma((NZ,)),
        dma((1,)),
        dma((NZ,)),
        dma((1,)),
        dma((3,)),
    ]
    whole = pl.BlockSpec(memory_space=pltpu.VMEM)
    update, grams = pl.pallas_call(
        functools.partial(kernel, layers, images, side, scale),
        out_shape=(
            jax.ShapeDtypeStruct((own_rows, width), F32),
            jax.ShapeDtypeStruct((2, width, width), F32),
        ),
        in_specs=[pl.BlockSpec(memory_space=pltpu.HBM)] * 4,
        out_specs=(whole, whole),
        scratch_shapes=scratch,
        compiler_params=pltpu.CompilerParams(
            collective_id=0, has_side_effects=True, vmem_limit_bytes=63 * 1024 * 1024
        ),
        name="kfac_step",
    )(
        layer_inputs.reshape(rows, width),
        output_grads.reshape(rows, width),
        input_inverse.transpose(1, 0, 2),
        grad_inverse.reshape(width, width),
    )
    return update[None], grams[None]


def solution(mesh):
    assert mesh.shape["pos"] == NX * NZ * NC and mesh.shape["layer"] % NY == 0
    return jax.shard_map(
        functools.partial(per_device, mesh.shape["layer"]),
        mesh=mesh,
        in_specs=(
            P("layer", "pos", None, None, None),
            P("layer", "pos", None, None, None),
            P("layer", "pos", None),
            P("layer", None, None),
        ),
        out_specs=(P("layer", "pos", None), P("layer", None, None, None)),
        check_vma=False,
    )
```

time: 93.3 us -> 80.6 us (0.86)
  Pallas kernels: 89.3 us -> 76.9 us
    pallas_call x1, Pallas kernels: 89.3 us -> 76.9 us  [per_device(): pl.pallas_call(functools.partial(kernel, layers, images, side, scale), ou...]
    unnamed x9 -> x2, local copies, waits for them, and re-layouts: 3.11 us -> 2.88 us
where the time goes in v2:
time: 80.6 us; the launch traced here: 80.4 us
  Pallas kernels  76.9 us (95%)
  local copies, waits for them, and re-layouts  2.88 us (4%)
    pallas_call x1, Pallas kernels, per_device(): pl.pallas_call(functools.partial(kernel, layers, images, side, scale), ou...  76.9 us
    unnamed x2, local copies, waits for them, and re-layouts  2.88 us

profile of v2, /device:TPU:25, one launch (start us, length us, event | category | flops | bytes accessed | tf_op | source)
XLA Modules:
  0.0 80.4 jit_solution(8192459013711128117)
XLA Ops:
  0.6 76.9 %kfac_step.1 = (f32[18,128]{1,0:T(8,128)}, f32[2,128,128]{2,1,0:T(8,128)}) custom-call(bf16[512,128]{1,0:T(8,128)(2,1)} %bitcast.6, bf16[512,128]{1,0:T(8,128)(2,1)} %bitcast.7, f32[18,1,1152]{2,1,0:T(1,128)} %bitcast.9, f32[128,128]{1,0:T(8,128)} %bitcast.10), custom_call_target="tpu_custom_call" | custom-call | tf_op jit(solution)/shard_map/kfac_step/pallas_call | solution.py:729
  77.5 1.3 %copy.6 = f32[1,18,128]{2,0,1:T(1,128)} copy(f32[1,18,128]{2,1,0:T(8,128)} %bitcast.11) | data formatting | bytes 18432
  78.9 1.6 %copy.8 = f32[1,2,128,128]{3,2,1,0:T(8,128)} copy(f32[1,2,128,128]{3,2,1,0:T(8,128)} %bitcast.8) | data formatting | bytes 262144

commit v3 on v2

--- a/solution.py
+++ b/solution.py
@@ -133,6 +133,7 @@
     up_send,
     up_recv,
     load_sem,
+    go_sem,
 ):
     layer = lax.axis_index("layer")
     pos = lax.axis_index("pos")
@@ -167,6 +168,8 @@
         return lax.rem(x + NX - dx, NX)
 
     other = NC - 1 - c
+    far_first = sorted(range(NZ), key=lambda pz: -abs(pz - ROOT))
+    others = far_first[:-1]
 
     loads = [
         pltpu.make_async_copy(src, dst, load_sem.at[i])
@@ -286,90 +289,77 @@
         for copy in copies:
             copy.wait_send()
 
-    def plane_start(kind, out, in_core):
-        copies = []
-        for dx in offsets() + [0]:
-            copy = rcopy(
+    def begin(copies):
+        for copy in copies:
+            copy.start()
+
+    def core_copies(kind, out, in_core):
+        return [
+            rcopy(
                 out.at[other * NX + ahead(dx)],
                 in_core.at[dx],
                 ex_send.at[kind, dx],
                 ex_recv.at[kind, dx],
                 dev(layer, x, z, other),
             )
-            copy.start()
-            copies.append(copy)
-        return copies
-
-    def plane_finish(kind, core_copies, part, in_core, out_x, in_x):
-        copies = []
-        for dx, arrival in zip(offsets(), core_copies):
-            arrival.wait_recv()
-            out_x[dx] = (part[c * NX + ahead(dx)] + in_core[dx].astype(F32)).astype(out_x.dtype)
-            copy = rcopy(
+            for dx in offsets() + [0]
+        ]
+
+    def x_copies(kind, out_x, in_x):
+        return [
+            rcopy(
                 out_x.at[dx],
                 in_x.at[dx],
                 ex_send.at[kind, NX + dx],
                 ex_recv.at[kind, NX + dx],
                 dev(layer, ahead(dx), z, c),
             )
+            for dx in offsets()
+        ]
+
+    def pass_on(core, along, part, in_core, out_x):
+        for dx, arrival, copy in zip(offsets(), core, along):
+            arrival.wait_recv()
+            out_x[dx] = (part[c * NX + ahead(dx)] + in_core[dx].astype(F32)).astype(out_x.dtype)
             copy.start()
-            copies.append(copy)
-        core_copies[-1].wait_recv()
+
+    def plane_total(core, along, part, in_core, in_x):
+        core[-1].wait_recv()
         total = part[strip] + in_core[0].astype(F32)
-        for dx, copy in reversed(list(zip(offsets(), copies))):
+        for dx, copy in reversed(list(zip(offsets(), along))):
             copy.wait_recv()
             total = total + in_x[dx].astype(F32)
-        return total, copies
+        return total
 
     def gather(kind, buf, own):
-        copies = []
-        for dx in offsets():
-            copies.append(
-                rcopy(
-                    buf.at[own],
-                    buf.at[own],
-                    ex_send.at[kind, dx],
-                    ex_recv.at[kind, dx],
-                    dev(layer, ahead(dx), z, c),
-                )
-            )
-        copies.append(
-            rcopy(
-                buf.at[own],
-                buf.at[own],
-                ex_send.at[kind, 0],
-                ex_recv.at[kind, 0],
-                dev(layer, x, z, other),
-            )
-        )
-        return copies
-
-    def gathered(kind, buf, place):
+        targets = [(dx, dev(layer, ahead(dx), z, c)) for dx in offsets()]
+        return [
+            rcopy(buf.at[own], buf.at[own], ex_send.at[kind, dx], ex_recv.at[kind, dx], to)
+            for dx, to in targets + [(0, dev(layer, x, z, other))]
+        ]
+
+    def passes(kind, buf, place):
         copies = []
         for dx in reversed(offsets()):
             got = buf.at[place(behind(dx), c)]
-            rcopy(
-                got, got, ex_send.at[kind, dx], ex_recv.at[kind, dx], dev(layer, x, z, other)
-            ).wait_recv()
-            copy = rcopy(
-                got,
-                got,
-                ex_send.at[kind, NX + dx],
-                ex_recv.at[kind, NX + dx],
-                dev(layer, x, z, other),
+            s = NX + dx
+            copies.append(
+                rcopy(got, got, ex_send.at[kind, s], ex_recv.at[kind, s], dev(layer, x, z, other))
             )
+        return copies
+
+    def arrival(kind, s, got):
+        rcopy(
+            got, got, ex_send.at[kind, s], ex_recv.at[kind, s], dev(layer, x, z, other)
+        ).wait_recv()
+
+    def gathered(kind, buf, place):
+        for dx, copy in zip(reversed(offsets()), passes(kind, buf, place)):
+            arrival(kind, dx, buf.at[place(behind(dx), c)])
             copy.start()
-            copies.append(copy)
-        for slot_of, dx in [(0, 0)] + [(NX + dx, dx) for dx in reversed(offsets())]:
-            got = buf.at[place(behind(dx), other)]
-            rcopy(
-                got,
-                got,
-                ex_send.at[kind, slot_of],
-                ex_recv.at[kind, slot_of],
-                dev(layer, x, z, other),
-            ).wait_recv()
-        return copies
+        arrival(kind, 0, buf.at[place(x, other)])
+        for dx in reversed(offsets()):
+            arrival(kind, NX + dx, buf.at[place(behind(dx), other)])
 
     def by_strip(px, pc):
         return pc * NX + px
@@ -401,10 +391,9 @@
     def root_total(z_slot, buf):
         total = plane_sum[...]
         src, dst = z_bufs[z_slot]
-        for pz in range(NZ):
-            if pz != ROOT:
-                z_arrived(z_slot, src, dst, pz)
-                total = total + dst[pz].astype(F32)
+        for pz in others:
+            z_arrived(z_slot, src, dst, pz)
+            total = total + dst[pz].astype(F32)
         buf[strip] = total * scale
 
     def fold(both):
@@ -419,8 +408,11 @@
         return fold(both[:, :width] + both[:, width:])
 
     part_one[...] = dot(grad_t[...], patches[...]).reshape(part_one.shape)
-    first = plane_start(0, part_one, in_one)
-    total, first_x = plane_finish(0, first, part_one, in_one, out_x_one, in_x_one)
+    first = core_copies(0, part_one, in_one)
+    first_x = x_copies(0, out_x_one, in_x_one)
+    begin(first)
+    pass_on(first, first_x, part_one, in_one, out_x_one)
+    total = plane_total(first, first_x, part_one, in_one, in_x_one)
     z_start(0, total)
 
     @pl.when(jnp.logical_not(has_next))
@@ -429,35 +421,69 @@
         pre[...] = jnp.zeros_like(pre)
 
     half_blocks = gram_part.shape[0] // 2
-
-    def grams():
+    gram_core = core_copies(2, gram_part, gram_in)
+    gram_x = x_copies(2, gram_out_x, gram_in_x)
+    gram_gather = gather(5, gram_full, strip)
+    bc_copies = [
+        rcopy(
+            gram_full.at[strip],
+            gram_full.at[strip],
+            bc_send.at[pz],
+            bc_recv.at[0],
+            dev(layer, x, pz, c),
+        )
+        for pz in others
+    ]
+
+    def gram_begin():
         arrived()
         shape = (half_blocks, gram_part.shape[1], width)
         gram_part[pl.ds(0, half_blocks)] = dot(grad_t[...], xg_ref[1]).reshape(shape)
         gram_part[pl.ds(half_blocks, half_blocks)] = dot(grad_t[...], xg_next[1]).reshape(shape)
-        copies = plane_start(2, gram_part, gram_in)
-        gram, copies_x = plane_finish(2, copies, gram_part, gram_in, gram_out_x, gram_in_x)
-        gram_z_out[...] = gram
-
-        @pl.when(is_rim)
-        def _():
-            z_copy(2, gram_z_out, gram_z_in).start()
-
-        sent(copies)
-        sent(copies_x)
-
-    @pl.when(jnp.logical_not(late))
-    def _():
-        grams()
-
-    @pl.when(sends_far)
-    def _():
-        far_own.start()
-
-    @pl.when(relays)
-    def _():
-        to_relay[0].wait_recv()
-        far_relay.start()
+        begin(gram_core)
+
+    def gram_pass():
+        pass_on(gram_core, gram_x, gram_part, gram_in, gram_out_x)
+
+    def gram_end():
+        gram_z_out[...] = plane_total(gram_core, gram_x, gram_part, gram_in, gram_in_x)
+
+    def gram_root():
+        total = gram_z_out[...]
+        for pz in others:
+            z_arrived(2, gram_z_out, gram_z_in, pz)
+            total = total + gram_z_in[pz]
+        gram_full[strip] = total * scale
+        begin(bc_copies)
+
+    def gram_send():
+        z_copy(2, gram_z_out, gram_z_in).start()
+
+    def far_start():
+        @pl.when(sends_far)
+        def _():
+            far_own.start()
+
+        @pl.when(relays)
+        def _():
+            to_relay[0].wait_recv()
+            far_relay.start()
+
+    early = jnp.logical_not(late)
+
+    @pl.when(early)
+    def _():
+        gram_begin()
+        gram_pass()
+
+    @pl.when(early & is_rim)
+    def _():
+        gram_end()
+
+    @pl.when(is_rim & (layer >= NY))
+    def _():
+        pl.semaphore_wait(go_sem, 1)
+        far_start()
 
     pre_copies = [
         rcopy(
@@ -467,11 +493,23 @@
             pre_recv.at[0],
             dev(layer - 1, x, pz, c),
         )
-        for pz in range(NZ)
+        for pz in far_first
     ]
 
     @pl.when(is_root)
     def _():
+        root_total(0, full_wide)
+        copies = gather(1, full_wide, strip)
+        begin(copies)
+
+        @pl.when(layer >= NY)
+        def _():
+            for pz in others:
+                pl.semaphore_signal(
+                    go_sem, inc=1, device_id=dev(layer, x, pz, c), device_id_type=MESH
+                )
+            far_start()
+
         for q in range(NZ):
             pltpu.make_async_copy(a_ref, a_in.at[q], a_recv.at[q]).wait()
             a_all[pl.ds(q * own_rows, own_rows), :] = a_in[q, :, 0, :]
@@ -479,26 +517,31 @@
         top = rows.astype(BF16)
         a_two[pl.ds(0, rows.shape[0]), :] = top
         a_two[pl.ds(rows.shape[0], rows.shape[0]), :] = (rows - top.astype(F32)).astype(BF16)
-        root_total(0, full_wide)
-        copies = gather(1, full_wide, strip)
-        for copy in copies:
-            copy.start()
-        passed = gathered(1, full_wide, by_strip)
+        gathered(1, full_wide, by_strip)
         value = dot(times_inverse(full_wide), ginv_ref[...], precision=HIGH)
         base[...] = value
         rows_full[...] = value.astype(BF16)
 
-        @pl.when(has_prev)
+        @pl.when(sends_near)
         def _():
             for copy in pre_copies:
                 copy.start()
 
+        @pl.when(sends_far)
+        def _():
+            for copy in reversed(pre_copies):
+                copy.start()
+
+        @pl.when(early)
+        def _():
+            gram_end()
+
         sent(copies)
-        sent(passed)
+        sent(passes(1, full_wide, by_strip))
 
     @pl.when(late)
     def _():
-        grams()
+        gram_begin()
 
     unfold(xg_next.at[0], patches_next, images, side, width)
 
@@ -508,99 +551,110 @@
             rows_full, pre.at[block], pre_send.at[0], pre_recv.at[0], dev(layer, x, z, other)
         ).wait_recv()
         copies = gather(3, pre, block)
-        for copy in copies:
-            copy.start()
-        passed = gathered(3, pre, by_block)
+        begin(copies)
+        gathered(3, pre, by_block)
         sent(copies)
-        sent(passed)
+        sent(passes(3, pre, by_block))
+
+    @pl.when(early & is_rim)
+    def _():
+        gram_send()
 
     mapped = dot(patches_next[...], pre[...].reshape(lanes, width)).astype(BF16)
     product = dot(mapped.T, patches[...])
     part[...] = product.reshape(part.shape)
     out_two[...] = product.astype(BF16).reshape(out_two.shape)
-    second = plane_start(4, out_two, in_two)
-    total, second_x = plane_finish(4, second, part, in_two, out_x_two, in_x_two)
+    second = core_copies(4, out_two, in_two)
+    second_x = x_copies(4, out_x_two, in_x_two)
+    begin(second)
+
+    @pl.when(late)
+    def _():
+        gram_pass()
+
+    pass_on(second, second_x, part, in_two, out_x_two)
+    total = plane_total(second, second_x, part, in_two, in_x_two)
     z_start(1, total)
 
-    bc_copies = [
-        rcopy(
-            gram_full.at[strip],
-            gram_full.at[strip],
-            bc_send.at[pz],
-            bc_recv.at[0],
-            dev(layer, x, pz, c),
-        )
-        for pz in range(NZ)
-    ]
-
-    gram_gather = gather(5, gram_full, strip)
-
-    @pl.when(is_rim)
-    def _():
-        bc_copies[ROOT].wait_recv()
-        for copy in gram_gather:
-            copy.start()
+    def gram_back():
+        @pl.when(is_root)
+        def _():
+            gram_root()
+
+        @pl.when(is_rim)
+        def _():
+            bc_copies[0].wait_recv()
+
+        begin(gram_gather)
+
+    @pl.when(late)
+    def _():
+        gram_end()
+
+    @pl.when(late & is_rim)
+    def _():
+        gram_send()
+
+    @pl.when(early)
+    def _():
+        gram_back()
+        gathered(5, gram_full, by_strip)
+
+    @pl.when(late & is_rim)
+    def _():
+        gram_back()
+        gathered(5, gram_full, by_strip)
 
     @pl.when(is_root)
     def _():
         root_total(1, full)
         copies = gather(6, full, strip)
-        for copy in copies:
-            copy.start()
-        total = gram_z_out[...]
-        for pz in range(NZ):
-            if pz != ROOT:
-                z_arrived(2, gram_z_out, gram_z_in, pz)
-                total = total + gram_z_in[pz]
-        gram_full[strip] = total * scale
-        for pz in range(NZ):
-            if pz != ROOT:
-                bc_copies[pz].start()
-        for copy in gram_gather:
-            copy.start()
-        passed = gathered(6, full, by_strip)
-        gram_passed = gathered(5, gram_full, by_strip)
+        begin(copies)
+
+        @pl.when(late)
+        def _():
+            gram_back()
+
+        gathered(6, full, by_strip)
+
+        @pl.when(late)
+        def _():
+            gathered(5, gram_full, by_strip)
+
         cross_gram = gram_full[pl.ds(half_blocks, half_blocks)].reshape(width, width)
         mix = dot(cross_gram, ginv_ref[...], (0, 0), HIGH)
         value = base[...] - dot(times_inverse(full), mix, precision=HIGH)
         result[...] = value
-        for q in range(NZ):
-            result_out[q] = result[pl.ds(q * own_rows, own_rows), :]
-            copy = rcopy(
+        up_copies = [
+            rcopy(
                 result_out.at[q],
                 result_in,
                 up_send.at[q],
                 up_recv.at[0],
                 dev(layer, x, c * per + q // NC, q % NC),
             )
-            if q // NC == ROOT % per and q % NC == ROOT // per:
-
-                @pl.when(c == ROOT // per)
-                def _(q=q):
-                    upd_ref[...] = result_out[q]
-
-                @pl.when(c != ROOT // per)
-                def _(copy=copy):
-                    copy.start()
-                    copy.wait_send()
-            else:
+            for q in range(NZ)
+        ]
+        own_q = (ROOT - c * per) * NC + c
+        for q in sorted(range(NZ), key=lambda q: -abs(q // NC - ROOT % per)):
+            result_out[q] = result[pl.ds(q * own_rows, own_rows), :]
+
+            @pl.when(own_q != q)
+            def _(copy=up_copies[q]):
                 copy.start()
-        for q in range(NZ):
-            if not (q // NC == ROOT % per and q % NC == ROOT // per):
-                rcopy(
-                    result_out.at[q],
-                    result_in,
-                    up_send.at[q],
-                    up_recv.at[0],
-                    dev(layer, x, c * per + q // NC, q % NC),
-                ).wait_send()
+
+        @pl.when(a_self)
+        def _():
+            upd_ref[...] = result_out[ROOT % per * NC + ROOT // per]
+
+        for q, copy in enumerate(up_copies):
+
+            @pl.when(own_q != q)
+            def _(copy=copy):
+                copy.wait_send()
+
         sent(copies)
-        sent(passed)
-        sent(gram_passed)
-
-    @pl.when(is_rim)
-    def _():
-        sent(gathered(5, gram_full, by_strip))
+        sent(passes(6, full, by_strip))
 
     gram_ref[...] = gram_full[...].reshape(gram_ref.shape)
 
@@ -615,7 +669,10 @@
     sent(first_x)
     sent(second)
     sent(second_x)
+    sent(gram_core)
+    sent(gram_x)
     sent(gram_gather)
+    sent(passes(5, gram_full, by_strip))
 
     @pl.when(a_other)
     def _():
@@ -643,9 +700,8 @@
 
     @pl.when(is_root)
     def _():
-        for pz in range(NZ):
-            if pz != ROOT:
-                bc_copies[pz].wait_send()
+        for copy in bc_copies:
+            copy.wait_send()
 
     @pl.when(is_root & has_prev)
     def _():
@@ -724,6 +780,7 @@
         dma((NZ,)),
         dma((1,)),
         dma((3,)),
+        pltpu.SemaphoreType.REGULAR,
     ]
     whole = pl.BlockSpec(memory_space=pltpu.VMEM)
     update, grams = pl.pallas_call(
@@ -736,14 +793,19 @@
         out_specs=(whole, whole),
         scratch_shapes=scratch,
         compiler_params=pltpu.CompilerParams(
-            collective_id=0, has_side_effects=True, vmem_limit_bytes=63 * 1024 * 1024
+            collective_id=0, has_side_effects=True, vmem_limit_bytes=48 * 1024 * 1024
         ),
         name="kfac_step",
     )(
-        layer_inputs.reshape(rows, width),
-        output_grads.reshape(rows, width),
-        input_inverse.transpose(1, 0, 2),
-        grad_inverse.reshape(width, width),
+        *(
+            pltpu.with_memory_space_constraint(value, pltpu.HBM)
+            for value in (
+                layer_inputs.reshape(rows, width),
+                output_grads.reshape(rows, width),
+                input_inverse.transpose(1, 0, 2),
+                grad_inverse.reshape(width, width),
+            )
+        )
     )
     return update[None], grams[None]
 

time: 80.6 us -> 76.6 us (0.950)
  Pallas kernels: 76.9 us -> 74.6 us
  local copies, waits for them, and re-layouts: 2.88 us -> 1.26 us
    pallas_call x1, Pallas kernels: 76.9 us -> 74.6 us  [per_device(): pl.pallas_call(functools.partial(kernel, layers, images, side, scale), ou...]
    unnamed x2, local copies, waits for them, and re-layouts: 2.88 us -> 1.26 us
where the time goes in v3:
time: 76.6 us; the launch traced here: 76.5 us
  Pallas kernels  74.6 us (97%)
  local copies, waits for them, and re-layouts  1.26 us (2%)
    pallas_call x1, Pallas kernels, per_device(): pl.pallas_call(functools.partial(kernel, layers, images, side, scale), ou...  74.6 us

profile of v3, /device:TPU:25, one launch (start us, length us, event | category | flops | bytes accessed | tf_op | source)
XLA Modules:
  0.0 76.5 jit_solution(13029533091112373878)
XLA Ops:
  0.6 74.6 %kfac_step.1 = (f32[18,128]{1,0:T(8,128)S(1)}, f32[2,128,128]{2,1,0:T(8,128)S(1)}) custom-call(bf16[512,128]{1,0:T(8,128)(2,1)} %bitcast.8, bf16[512,128]{1,0:T(8,128)(2,1)} %bitcast.9, f32[18,1,1152]{2,1,0:T(1,128)} %bitcast.10, f32[128,128]{1,0:T(8,128)} %bitcast.11), custom_call_target="tpu_custom_call" | custom-call | tf_op jit(solution)/shard_map/kfac_step/pallas_call | solution.py:786
  75.2 0.6 copy.6
  75.8 0.7 copy.8

commit v4 on v3

--- a/solution.py
+++ b/solution.py
@@ -134,6 +134,7 @@
     up_recv,
     load_sem,
     go_sem,
+    ready_sem,
 ):
     layer = lax.axis_index("layer")
     pos = lax.axis_index("pos")
@@ -183,38 +184,38 @@
     def greet(to):
         pl.semaphore_signal(barrier, inc=1, device_id=to, device_id_type=MESH)
 
-    greet(dev(layer, x, z, other))
+    @pl.when(c != 0)
+    def _():
+        greet(dev(layer, x, z, 0))
+
     for dx in offsets():
-        greet(dev(layer, ahead(dx), z, c))
+        greet(dev(layer, ahead(dx), z, 0))
 
     @pl.when(is_rim)
     def _():
-        for pc in range(NC):
-            greet(dev(layer, x, ROOT, pc))
+        greet(dev(layer, x, ROOT, 0))
 
     @pl.when(is_root)
     def _():
-        for pz in range(NZ):
-            if pz != ROOT:
-                for pc in range(NC):
-                    greet(dev(layer, x, pz, pc))
+        for pz in others:
+            greet(dev(layer, x, pz, 0))
 
     @pl.when(has_next)
     def _():
-        greet(dev(layer + 1, x, z, c))
+        greet(dev(layer + 1, x, z, 1))
 
     @pl.when(has_next & is_rim)
     def _():
-        greet(dev(layer + 1, x, ROOT, c))
+        greet(dev(layer + 1, x, ROOT, 1))
 
     @pl.when(relays)
     def _():
-        greet(dev(layer - y, x, z, c))
+        greet(dev(layer - y, x, z, 1))
 
     @pl.when(late)
     def _():
         for q in range(1, NY):
-            greet(dev(layer + 1 + q, x, z, c))
+            greet(dev(layer + 1 + q, x, z, 1))
 
     for load in loads:
         load.wait()
@@ -222,10 +223,21 @@
     grad_t[...] = xg_ref[1].T
 
     root = is_root.astype(jnp.int32)
-    prv = has_prev.astype(jnp.int32)
-    expected = NX + prv + sends_far.astype(jnp.int32) * (NY - 1) + relays.astype(jnp.int32)
-    expected = expected + root * ((NZ - 1) * NC + prv * (NZ - 1)) + (1 - root) * NC
-    pl.semaphore_wait(barrier, expected)
+    chips = 1 + root * (NZ - 2)
+    near_greets = 1 + NC * (NX - 1 + chips)
+    chips = 1 + root * (NZ - 1) + sends_far.astype(jnp.int32) * (NY - 1) + relays.astype(jnp.int32)
+    far_greets = NC * chips
+
+    @pl.when(c == 0)
+    def _():
+        pl.semaphore_wait(barrier, near_greets)
+        pl.semaphore_signal(
+            ready_sem, inc=1, device_id=dev(layer, x, z, other), device_id_type=MESH
+        )
+
+    @pl.when(c != 0)
+    def _():
+        pl.semaphore_wait(ready_sem, 1)
 
     shift = rcopy(xg_ref, xg_next, shift_send.at[0], shift_recv.at[0], dev(layer - 1, x, z, c))
 
@@ -276,15 +288,6 @@
     def _():
         a_local.start()
 
-    @pl.when(sends_near)
-    def _():
-        shift.start()
-
-    @pl.when(sends_far)
-    def _():
-        for copy in to_relay:
-            copy.start()
-
     def sent(copies):
         for copy in copies:
             copy.wait_send()
@@ -412,6 +415,27 @@
     first_x = x_copies(0, out_x_one, in_x_one)
     begin(first)
     pass_on(first, first_x, part_one, in_one, out_x_one)
+
+    @pl.when(has_prev & (c != 0))
+    def _():
+        pl.semaphore_wait(barrier, far_greets)
+        pl.semaphore_signal(
+            ready_sem, inc=1, device_id=dev(layer, x, z, other), device_id_type=MESH
+        )
+
+    @pl.when(has_prev & (c == 0))
+    def _():
+        pl.semaphore_wait(ready_sem, 1)
+
+    @pl.when(sends_near)
+    def _():
+        shift.start()
+
+    @pl.when(sends_far)
+    def _():
+        for copy in to_relay:
+            copy.start()
+
     total = plane_total(first, first_x, part_one, in_one, in_x_one)
     z_start(0, total)
 
@@ -499,8 +523,7 @@
     @pl.when(is_root)
     def _():
         root_total(0, full_wide)
-        copies = gather(1, full_wide, strip)
-        begin(copies)
+        begin(gather(1, full_wide, strip))
 
         @pl.when(layer >= NY)
         def _():
@@ -536,8 +559,6 @@
         def _():
             gram_end()
 
-        sent(copies)
-        sent(passes(1, full_wide, by_strip))
 
     @pl.when(late)
     def _():
@@ -550,11 +571,8 @@
         rcopy(
             rows_full, pre.at[block], pre_send.at[0], pre_recv.at[0], dev(layer, x, z, other)
         ).wait_recv()
-        copies = gather(3, pre, block)
-        begin(copies)
+        begin(gather(3, pre, block))
         gathered(3, pre, by_block)
-        sent(copies)
-        sent(passes(3, pre, by_block))
 
     @pl.when(early & is_rim)
     def _():
@@ -605,11 +623,22 @@
         gram_back()
         gathered(5, gram_full, by_strip)
 
+    up_copies = [
+        rcopy(
+            result_out.at[q],
+            result_in,
+            up_send.at[q],
+            up_recv.at[0],
+            dev(layer, x, c * per + q // NC, q % NC),
+        )
+        for q in range(NZ)
+    ]
+    own_q = (ROOT - c * per) * NC + c
+
     @pl.when(is_root)
     def _():
         root_total(1, full)
-        copies = gather(6, full, strip)
-        begin(copies)
+        begin(gather(6, full, strip))
 
         @pl.when(late)
         def _():
@@ -625,17 +654,6 @@
         mix = dot(cross_gram, ginv_ref[...], (0, 0), HIGH)
         value = base[...] - dot(times_inverse(full), mix, precision=HIGH)
         result[...] = value
-        up_copies = [
-            rcopy(
-                result_out.at[q],
-                result_in,
-                up_send.at[q],
-                up_recv.at[0],
-                dev(layer, x, c * per + q // NC, q % NC),
-            )
-            for q in range(NZ)
-        ]
-        own_q = (ROOT - c * per) * NC + c
         for q in sorted(range(NZ), key=lambda q: -abs(q // NC - ROOT % per)):
             result_out[q] = result[pl.ds(q * own_rows, own_rows), :]
 
@@ -646,15 +664,6 @@
         @pl.when(a_self)
         def _():
             upd_ref[...] = result_out[ROOT % per * NC + ROOT // per]
-
-        for q, copy in enumerate(up_copies):
-
-            @pl.when(own_q != q)
-            def _(copy=copy):
-                copy.wait_send()
-
-        sent(copies)
-        sent(passes(6, full, by_strip))
 
     gram_ref[...] = gram_full[...].reshape(gram_ref.shape)
 
@@ -700,8 +709,20 @@
 
     @pl.when(is_root)
     def _():
-        for copy in bc_copies:
-            copy.wait_send()
+        sent(bc_copies)
+        for kind, buf in ((1, full_wide), (6, full)):
+            sent(gather(kind, buf, strip))
+            sent(passes(kind, buf, by_strip))
+        for q, copy in enumerate(up_copies):
+
+            @pl.when(own_q != q)
+            def _(copy=copy):
+                copy.wait_send()
+
+    @pl.when(has_next)
+    def _():
+        sent(gather(3, pre, block))
+        sent(passes(3, pre, by_block))
 
     @pl.when(is_root & has_prev)
     def _():
@@ -781,6 +802,7 @@
         dma((1,)),
         dma((3,)),
         pltpu.SemaphoreType.REGULAR,
+        pltpu.SemaphoreType.REGULAR,
     ]
     whole = pl.BlockSpec(memory_space=pltpu.VMEM)
     update, grams = pl.pallas_call(

time: 76.6 us -> 75.3 us (0.983)
  Pallas kernels: 74.6 us -> 73.3 us
    pallas_call x1, Pallas kernels: 74.6 us -> 73.3 us  [per_device(): pl.pallas_call(functools.partial(kernel, layers, images, side, scale), ou...]
where the time goes in v4:
time: 75.3 us; the launch traced here: 75.2 us
  Pallas kernels  73.3 us (97%)
  local copies, waits for them, and re-layouts  1.26 us (2%)
    pallas_call x1, Pallas kernels, per_device(): pl.pallas_call(functools.partial(kernel, layers, images, side, scale), ou...  73.3 us

profile of v4, /device:TPU:25, one launch (start us, length us, event | category | flops | bytes accessed | tf_op | source)
XLA Modules:
  0.0 75.2 jit_solution(6699440095223365045)
XLA Ops:
  0.6 73.3 %kfac_step.1 = (f32[18,128]{1,0:T(8,128)S(1)}, f32[2,128,128]{2,1,0:T(8,128)S(1)}) custom-call(bf16[512,128]{1,0:T(8,128)(2,1)} %bitcast.8, bf16[512,128]{1,0:T(8,128)(2,1)} %bitcast.9, f32[18,1,1152]{2,1,0:T(1,128)} %bitcast.10, f32[128,128]{1,0:T(8,128)} %bitcast.11), custom_call_target="tpu_custom_call" | custom-call | tf_op jit(solution)/shard_map/kfac_step/pallas_call | solution.py:808
  73.9 0.6 copy.6
  74.5 0.7 copy.8

commit v5 on v4

--- a/solution.py
+++ b/solution.py
@@ -29,6 +29,12 @@
         device_id=to,
         device_id_type=MESH,
     )
+
+
+def part_of(rows, q):
+    size = -(-rows // (NY - 1) // 16) * 16
+    start = (q - 1) * size
+    return start, min(size, rows - start)
 
 
 def dot(a, b, contract=(1, 0), precision=None):
@@ -133,7 +139,6 @@
     up_send,
     up_recv,
     load_sem,
-    go_sem,
     ready_sem,
 ):
     layer = lax.axis_index("layer")
@@ -145,7 +150,6 @@
     strip = c * NX + x
     n = NX * NC
     _, rows, width = xg_ref.shape
-    quarter = rows // NY
     y = lax.rem(layer, NY)
     lanes = TAPS * width
     per = NZ // NC
@@ -240,26 +244,27 @@
         pl.semaphore_wait(ready_sem, 1)
 
     shift = rcopy(xg_ref, xg_next, shift_send.at[0], shift_recv.at[0], dev(layer - 1, x, z, c))
+    hops = range(1, NY)
 
     def piece(ref, q):
-        return ref.at[:, pl.ds(pl.multiple_of(q * quarter, quarter), quarter)]
+        start, size = part_of(rows, q)
+        return ref.at[:, pl.ds(start, size)]
+
+    def held(q):
+        return relay.at[:, pl.ds(0, part_of(rows, q)[1])]
 
     to_relay = [
         rcopy(
-            piece(xg_ref, q),
-            relay,
-            relay_send.at[q],
-            relay_recv.at[0],
-            dev(layer + q, x, z, c),
+            piece(xg_ref, q), held(q), relay_send.at[q], relay_recv.at[0], dev(layer + q, x, z, c)
         )
-        for q in range(1, NY)
+        for q in hops
     ]
-    far_own = rcopy(
-        piece(xg_ref, 0), piece(xg_next, 0), far_send.at[0], far_recv.at[0], dev(layer - 1, x, z, c)
-    )
-    far_relay = rcopy(
-        relay, piece(xg_next, y), far_send.at[0], far_recv.at[y], dev(layer - y - 1, x, z, c)
-    )
+    far_relay = [
+        rcopy(
+            held(q), piece(xg_next, q), far_send.at[0], far_recv.at[q], dev(layer - q - 1, x, z, c)
+        )
+        for q in hops
+    ]
 
     def arrived():
         @pl.when(has_next & jnp.logical_not(late))
@@ -268,10 +273,8 @@
 
         @pl.when(late)
         def _():
-            for q in range(NY):
-                rcopy(
-                    relay, piece(xg_next, q), far_send.at[0], far_recv.at[q], dev(layer, x, z, other)
-                ).wait_recv()
+            for copy in far_relay:
+                copy.wait_recv()
 
     half = lax.div(z, per)
     slot = lax.rem(z, per) * NC + c
@@ -438,6 +441,14 @@
 
     total = plane_total(first, first_x, part_one, in_one, in_x_one)
     z_start(0, total)
+
+    for q in hops:
+
+        @pl.when(relays & (y == q))
+        def _(q=q):
+            to_relay[q - 1].wait_recv()
+            far_relay[q - 1].start()
+
 
     @pl.when(jnp.logical_not(has_next))
     def _():
@@ -483,16 +494,6 @@
     def gram_send():
         z_copy(2, gram_z_out, gram_z_in).start()
 
-    def far_start():
-        @pl.when(sends_far)
-        def _():
-            far_own.start()
-
-        @pl.when(relays)
-        def _():
-            to_relay[0].wait_recv()
-            far_relay.start()
-
     early = jnp.logical_not(late)
 
     @pl.when(early)
@@ -503,11 +504,6 @@
     @pl.when(early & is_rim)
     def _():
         gram_end()
-
-    @pl.when(is_rim & (layer >= NY))
-    def _():
-        pl.semaphore_wait(go_sem, 1)
-        far_start()
 
     pre_copies = [
         rcopy(
@@ -524,14 +520,6 @@
     def _():
         root_total(0, full_wide)
         begin(gather(1, full_wide, strip))
-
-        @pl.when(layer >= NY)
-        def _():
-            for pz in others:
-                pl.semaphore_signal(
-                    go_sem, inc=1, device_id=dev(layer, x, pz, c), device_id_type=MESH
-                )
-            far_start()
 
         for q in range(NZ):
             pltpu.make_async_copy(a_ref, a_in.at[q], a_recv.at[q]).wait()
@@ -695,11 +683,12 @@
     def _():
         for copy in to_relay:
             copy.wait_send()
-        far_own.wait_send()
-
-    @pl.when(relays)
-    def _():
-        far_relay.wait_send()
+
+    for q in hops:
+
+        @pl.when(relays & (y == q))
+        def _(q=q):
+            far_relay[q - 1].wait_send()
 
     @pl.when(is_rim)
     def _():
@@ -749,7 +738,7 @@
         vmem((rows, lanes), BF16),
         vmem((width, rows), BF16),
         vmem((2, rows, width), BF16),
-        vmem((2, rows // NY, width), BF16),
+        vmem((2, part_of(rows, 1)[1], width), BF16),
         vmem((n, strip, lanes), F32),
         vmem((n, strip, lanes), F32),
         vmem((NX, strip, lanes), F32),
@@ -802,7 +791,6 @@
         dma((1,)),
         dma((3,)),
         pltpu.SemaphoreType.REGULAR,
-        pltpu.SemaphoreType.REGULAR,
     ]
     whole = pl.BlockSpec(memory_space=pltpu.VMEM)
     update, grams = pl.pallas_call(

time: 75.3 us -> 74.5 us (0.989)
  Pallas kernels: 73.3 us -> 72.4 us
    pallas_call x1, Pallas kernels: 73.3 us -> 72.4 us  [per_device(): pl.pallas_call(functools.partial(kernel, layers, images, side, scale), ou...]
where the time goes in v5:
time: 74.5 us; the launch traced here: 74.3 us
  Pallas kernels  72.4 us (97%)
  local copies, waits for them, and re-layouts  1.26 us (2%)
    pallas_call x1, Pallas kernels, per_device(): pl.pallas_call(functools.partial(kernel, layers, images, side, scale), ou...  72.4 us

profile of v5, /device:TPU:25, one launch (start us, length us, event | category | flops | bytes accessed | tf_op | source)
XLA Modules:
  0.0 74.3 jit_solution(11320159889617048332)
XLA Ops:
  0.6 72.4 %kfac_step.1 = (f32[18,128]{1,0:T(8,128)S(1)}, f32[2,128,128]{2,1,0:T(8,128)S(1)}) custom-call(bf16[512,128]{1,0:T(8,128)(2,1)} %bitcast.8, bf16[512,128]{1,0:T(8,128)(2,1)} %bitcast.9, f32[18,1,1152]{2,1,0:T(1,128)} %bitcast.10, f32[128,128]{1,0:T(8,128)} %bitcast.11), custom_call_target="tpu_custom_call" | custom-call | tf_op jit(solution)/shard_map/kfac_step/pallas_call | solution.py:796
  73.1 0.6 copy.6
  73.7 0.7 copy.8

commit v6 on v5

--- a/solution.py
+++ b/solution.py
@@ -140,6 +140,7 @@
     up_recv,
     load_sem,
     ready_sem,
+    go_sem,
 ):
     layer = lax.axis_index("layer")
     pos = lax.axis_index("pos")
@@ -154,6 +155,9 @@
     lanes = TAPS * width
     per = NZ // NC
     own_rows = result_in.shape[0]
+    front = (TAPS + 1) // 2 * width
+    spans = ((0, front, 0), (front, lanes - front, 1))
+    narrow = (0, width, 0)
     is_root = z == ROOT
     is_rim = z != ROOT
     has_next = layer < layers - 1
@@ -255,7 +259,7 @@
 
     to_relay = [
         rcopy(
-            piece(xg_ref, q), held(q), relay_send.at[q], relay_recv.at[0], dev(layer + q, x, z, c)
+            piece(xg_ref, q), held(q), relay_send.at[0], relay_recv.at[0], dev(layer + q, x, z, c)
         )
         for q in hops
     ]
@@ -280,10 +284,12 @@
     slot = lax.rem(z, per) * NC + c
     a_self = is_root & (half == c)
     a_other = jnp.logical_not(a_self)
-    a_remote = rcopy(a_ref, a_in.at[slot], a_send.at[0], a_recv.at[slot], dev(layer, x, ROOT, half))
-    a_local = pltpu.make_async_copy(a_ref, a_in.at[slot], a_recv.at[slot])
-
-    @pl.when(a_other)
+    held_back = (z > ROOT) & (z <= ROOT + 2)
+    group = lax.div(slot, NZ // 2)
+    a_remote = rcopy(a_ref, a_in.at[slot], a_send.at[0], a_recv.at[group], dev(layer, x, ROOT, half))
+    a_local = pltpu.make_async_copy(a_ref, a_in.at[slot], a_recv.at[group])
+
+    @pl.when(a_other & jnp.logical_not(held_back))
     def _():
         a_remote.start()
 
@@ -291,9 +297,8 @@
     def _():
         a_local.start()
 
-    def sent(copies):
-        for copy in copies:
-            copy.wait_send()
+    def cols(view, span):
+        return view.at[:, pl.ds(span[0], span[1])]
 
     def begin(copies):
         for copy in copies:
@@ -304,68 +309,77 @@
             rcopy(
                 out.at[other * NX + ahead(dx)],
                 in_core.at[dx],
-                ex_send.at[kind, dx],
+                ex_send.at[kind, 0],
                 ex_recv.at[kind, dx],
                 dev(layer, x, z, other),
             )
             for dx in offsets() + [0]
         ]
 
-    def x_copies(kind, out_x, in_x):
+    def x_copies(kind, out_x, in_x, span):
         return [
             rcopy(
-                out_x.at[dx],
-                in_x.at[dx],
-                ex_send.at[kind, NX + dx],
-                ex_recv.at[kind, NX + dx],
+                cols(out_x.at[dx], span),
+                cols(in_x.at[dx], span),
+                ex_send.at[kind, 1],
+                ex_recv.at[kind, NX + span[2]],
                 dev(layer, ahead(dx), z, c),
             )
             for dx in offsets()
         ]
 
-    def pass_on(core, along, part, in_core, out_x):
+    def pass_on(core, along, part, in_core, out_x, span):
+        at = pl.ds(span[0], span[1])
         for dx, arrival, copy in zip(offsets(), core, along):
-            arrival.wait_recv()
-            out_x[dx] = (part[c * NX + ahead(dx)] + in_core[dx].astype(F32)).astype(out_x.dtype)
+            if span[2] == 0:
+                arrival.wait_recv()
+            mine = part[c * NX + ahead(dx), :, at]
+            out_x[dx, :, at] = (mine + in_core[dx, :, at].astype(F32)).astype(out_x.dtype)
             copy.start()
 
-    def plane_total(core, along, part, in_core, in_x):
-        core[-1].wait_recv()
-        total = part[strip] + in_core[0].astype(F32)
-        for dx, copy in reversed(list(zip(offsets(), along))):
-            copy.wait_recv()
-            total = total + in_x[dx].astype(F32)
+    def plane_total(kind, core, part, in_core, in_x, span):
+        at = pl.ds(span[0], span[1])
+        if span[2] == 0:
+            core[-1].wait_recv()
+        total = part[strip, :, at] + in_core[0, :, at].astype(F32)
+        got = in_x.at[pl.ds(1, NX - 1), :, at]
+        rcopy(
+            got, got, ex_send.at[kind, 1], ex_recv.at[kind, NX + span[2]], dev(layer, x, z, other)
+        ).wait_recv()
+        for dx in range(1, NX):
+            total = total + in_x[dx, :, at].astype(F32)
         return total
 
-    def gather(kind, buf, own):
+    def all_sent(sem, view):
+        rcopy(view, view, sem, ex_recv.at[0, 0], dev(layer, x, z, other)).wait_send()
+
+    def plane_sent(kind, in_core, in_x):
+        all_sent(ex_send.at[kind, 0], in_core)
+        all_sent(ex_send.at[kind, 1], in_x.at[pl.ds(1, NX - 1)])
+
+    def gather_sent(kind, buf):
+        all_sent(ex_send.at[kind, 0], buf.at[pl.ds(0, NX)])
+        all_sent(ex_send.at[kind, 1], buf.at[pl.ds(0, NX - 1)])
+
+    def crossing(kind, out, s, got, to):
+        return rcopy(got, got, ex_send.at[kind, out], ex_recv.at[kind, s], to)
+
+    def gather(kind, buf, own, span):
         targets = [(dx, dev(layer, ahead(dx), z, c)) for dx in offsets()]
+        got = cols(buf.at[own], span)
         return [
-            rcopy(buf.at[own], buf.at[own], ex_send.at[kind, dx], ex_recv.at[kind, dx], to)
+            crossing(kind, 0, NX * span[2] + dx, got, to)
             for dx, to in targets + [(0, dev(layer, x, z, other))]
         ]
 
-    def passes(kind, buf, place):
-        copies = []
+    def gathered(kind, buf, place, span):
+        partner = dev(layer, x, z, other)
         for dx in reversed(offsets()):
-            got = buf.at[place(behind(dx), c)]
-            s = NX + dx
-            copies.append(
-                rcopy(got, got, ex_send.at[kind, s], ex_recv.at[kind, s], dev(layer, x, z, other))
-            )
-        return copies
-
-    def arrival(kind, s, got):
-        rcopy(
-            got, got, ex_send.at[kind, s], ex_recv.at[kind, s], dev(layer, x, z, other)
-        ).wait_recv()
-
-    def gathered(kind, buf, place):
-        for dx, copy in zip(reversed(offsets()), passes(kind, buf, place)):
-            arrival(kind, dx, buf.at[place(behind(dx), c)])
-            copy.start()
-        arrival(kind, 0, buf.at[place(x, other)])
-        for dx in reversed(offsets()):
-            arrival(kind, NX + dx, buf.at[place(behind(dx), other)])
+            got = cols(buf.at[place(behind(dx), c)], span)
+            crossing(kind, 0, NX * span[2] + dx, got, partner).wait_recv()
+            crossing(kind, 1, NX * span[2], got, partner).start()
+        got = buf.at[pl.ds(0, NX), :, pl.ds(span[0], span[1])]
+        crossing(kind, 0, NX * span[2], got, partner).wait_recv()
 
     def by_strip(px, pc):
         return pc * NX + px
@@ -373,34 +387,39 @@
     def by_block(px, pc):
         return px * NC + pc
 
-    def z_copy(kind, src, dst):
+    def z_copy(kind, src, dst, span):
         return rcopy(
-            src, dst.at[z], z_send.at[kind], z_recv.at[kind, z], dev(layer, x, ROOT, c)
+            cols(src, span),
+            cols(dst.at[z], span),
+            z_send.at[kind],
+            z_recv.at[kind, span[2]],
+            dev(layer, x, ROOT, c),
         )
 
-    def z_arrived(kind, src, dst, pz):
-        rcopy(
-            src, dst.at[pz], z_send.at[kind], z_recv.at[kind, pz], dev(layer, x, ROOT, c)
-        ).wait_recv()
+    def z_arrived(kind, dst, span):
+        got = dst.at[pl.ds(0, NZ - 1), :, pl.ds(span[0], span[1])]
+        rcopy(got, got, z_send.at[kind], z_recv.at[kind, span[2]], dev(layer, x, z, other)).wait_recv()
 
     z_bufs = ((z_out_wide, z_in_wide), (z_out, z_in))
 
-    def z_start(z_slot, total):
-        plane_sum[...] = total
+    def z_start(z_slot, total, span):
+        at = pl.ds(span[0], span[1])
+        plane_sum[:, at] = total
         src, dst = z_bufs[z_slot]
 
         @pl.when(is_rim)
         def _():
-            src[...] = total.astype(src.dtype)
-            z_copy(z_slot, src, dst).start()
-
-    def root_total(z_slot, buf):
-        total = plane_sum[...]
-        src, dst = z_bufs[z_slot]
+            src[:, at] = total.astype(src.dtype)
+            z_copy(z_slot, src, dst, span).start()
+
+    def root_total(z_slot, buf, span):
+        at = pl.ds(span[0], span[1])
+        total = plane_sum[:, at]
+        _, dst = z_bufs[z_slot]
+        z_arrived(z_slot, dst, span)
         for pz in others:
-            z_arrived(z_slot, src, dst, pz)
-            total = total + dst[pz].astype(F32)
-        buf[strip] = total * scale
+            total = total + dst[pz, :, at].astype(F32)
+        buf[strip, :, at] = total * scale
 
     def fold(both):
         half_rows = both.shape[0] // 2
@@ -415,9 +434,10 @@
 
     part_one[...] = dot(grad_t[...], patches[...]).reshape(part_one.shape)
     first = core_copies(0, part_one, in_one)
-    first_x = x_copies(0, out_x_one, in_x_one)
+    first_x = [x_copies(0, out_x_one, in_x_one, span) for span in spans]
     begin(first)
-    pass_on(first, first_x, part_one, in_one, out_x_one)
+    for span, along in zip(spans, first_x):
+        pass_on(first, along, part_one, in_one, out_x_one, span)
 
     @pl.when(has_prev & (c != 0))
     def _():
@@ -439,8 +459,8 @@
         for copy in to_relay:
             copy.start()
 
-    total = plane_total(first, first_x, part_one, in_one, in_x_one)
-    z_start(0, total)
+    for span in spans:
+        z_start(0, plane_total(0, first, part_one, in_one, in_x_one, span), span)
 
     for q in hops:
 
@@ -457,13 +477,13 @@
 
     half_blocks = gram_part.shape[0] // 2
     gram_core = core_copies(2, gram_part, gram_in)
-    gram_x = x_copies(2, gram_out_x, gram_in_x)
-    gram_gather = gather(5, gram_full, strip)
+    gram_x = x_copies(2, gram_out_x, gram_in_x, narrow)
+    gram_gather = gather(5, gram_full, strip, narrow)
     bc_copies = [
         rcopy(
             gram_full.at[strip],
             gram_full.at[strip],
-            bc_send.at[pz],
+            bc_send.at[0],
             bc_recv.at[0],
             dev(layer, x, pz, c),
         )
@@ -478,21 +498,21 @@
         begin(gram_core)
 
     def gram_pass():
-        pass_on(gram_core, gram_x, gram_part, gram_in, gram_out_x)
+        pass_on(gram_core, gram_x, gram_part, gram_in, gram_out_x, narrow)
 
     def gram_end():
-        gram_z_out[...] = plane_total(gram_core, gram_x, gram_part, gram_in, gram_in_x)
+        gram_z_out[...] = plane_total(2, gram_core, gram_part, gram_in, gram_in_x, narrow)
 
     def gram_root():
         total = gram_z_out[...]
+        z_arrived(2, gram_z_in, narrow)
         for pz in others:
-            z_arrived(2, gram_z_out, gram_z_in, pz)
             total = total + gram_z_in[pz]
         gram_full[strip] = total * scale
         begin(bc_copies)
 
     def gram_send():
-        z_copy(2, gram_z_out, gram_z_in).start()
+        z_copy(2, gram_z_out, gram_z_in, narrow).start()
 
     early = jnp.logical_not(late)
 
@@ -504,31 +524,48 @@
     @pl.when(early & is_rim)
     def _():
         gram_end()
+
+    @pl.when(held_back)
+    def _():
+        pl.semaphore_wait(go_sem, 1)
+        a_remote.start()
 
     pre_copies = [
         rcopy(
             rows_full,
             pre.at[block],
-            pre_send.at[pz],
+            pre_send.at[0],
             pre_recv.at[0],
             dev(layer - 1, x, pz, c),
         )
         for pz in far_first
     ]
 
+    def assemble(g):
+        taken = a_in.at[pl.ds(g * (NZ // 2), NZ // 2)]
+        pltpu.make_async_copy(taken, taken, a_recv.at[g]).wait()
+        for q in range(g * (NZ // 2), (g + 1) * (NZ // 2)):
+            a_all[pl.ds(q * own_rows, own_rows), :] = a_in[q, :, 0, :]
+
     @pl.when(is_root)
     def _():
-        root_total(0, full_wide)
-        begin(gather(1, full_wide, strip))
-
-        for q in range(NZ):
-            pltpu.make_async_copy(a_ref, a_in.at[q], a_recv.at[q]).wait()
-            a_all[pl.ds(q * own_rows, own_rows), :] = a_in[q, :, 0, :]
+        root_total(0, full_wide, spans[0])
+        begin(gather(1, full_wide, strip, spans[0]))
+        for d in range(2):
+            pl.semaphore_signal(
+                go_sem, inc=1, device_id=dev(layer, x, ROOT + 1 + d, c), device_id_type=MESH
+            )
+        root_total(0, full_wide, spans[1])
+        begin(gather(1, full_wide, strip, spans[1]))
+
+        assemble(1)
+        for span in spans:
+            gathered(1, full_wide, by_strip, span)
+        assemble(0)
         rows = a_all[...]
         top = rows.astype(BF16)
         a_two[pl.ds(0, rows.shape[0]), :] = top
         a_two[pl.ds(rows.shape[0], rows.shape[0]), :] = (rows - top.astype(F32)).astype(BF16)
-        gathered(1, full_wide, by_strip)
         value = dot(times_inverse(full_wide), ginv_ref[...], precision=HIGH)
         base[...] = value
         rows_full[...] = value.astype(BF16)
@@ -559,8 +596,8 @@
         rcopy(
             rows_full, pre.at[block], pre_send.at[0], pre_recv.at[0], dev(layer, x, z, other)
         ).wait_recv()
-        begin(gather(3, pre, block))
-        gathered(3, pre, by_block)
+        begin(gather(3, pre, block, narrow))
+        gathered(3, pre, by_block, narrow)
 
     @pl.when(early & is_rim)
     def _():
@@ -571,17 +608,17 @@
     part[...] = product.reshape(part.shape)
     out_two[...] = product.astype(BF16).reshape(out_two.shape)
     second = core_copies(4, out_two, in_two)
-    second_x = x_copies(4, out_x_two, in_x_two)
+    second_x = [x_copies(4, out_x_two, in_x_two, span) for span in spans]
     begin(second)
 
     @pl.when(late)
     def _():
         gram_pass()
 
-    pass_on(second, second_x, part, in_two, out_x_two)
-    total = plane_total(second, second_x, part, in_two, in_x_two)
-    z_start(1, total)
-
+    for span, along in zip(spans, second_x):
+        pass_on(second, along, part, in_two, out_x_two, span)
+    for span in spans:
+        z_start(1, plane_total(4, second, part, in_two, in_x_two, span), span)
     def gram_back():
         @pl.when(is_root)
         def _():
@@ -604,18 +641,63 @@
     @pl.when(early)
     def _():
         gram_back()
-        gathered(5, gram_full, by_strip)
+        gathered(5, gram_full, by_strip, narrow)
 
     @pl.when(late & is_rim)
     def _():
         gram_back()
-        gathered(5, gram_full, by_strip)
+        gathered(5, gram_full, by_strip, narrow)
+
+    @pl.when(is_rim | early)
+    def _():
+        gram_ref[...] = gram_full[...].reshape(gram_ref.shape)
+
+    plane_sent(0, in_one, in_x_one)
+    plane_sent(2, gram_in, gram_in_x)
+    plane_sent(4, in_two, in_x_two)
+
+    @pl.when(a_other)
+    def _():
+        a_remote.wait_send()
+
+    @pl.when(sends_near)
+    def _():
+        shift.wait_send()
+
+    @pl.when(sends_far)
+    def _():
+        all_sent(relay_send.at[0], xg_next)
+
+    for q in hops:
+
+        @pl.when(relays & (y == q))
+        def _(q=q):
+            far_relay[q - 1].wait_send()
+
+    @pl.when(has_next)
+    def _():
+        gather_sent(3, pre)
+
+    @pl.when(is_root & has_prev)
+    def _():
+        all_sent(pre_send.at[0], pre)
+
+    @pl.when(is_root)
+    def _():
+        gather_sent(1, full_wide)
+
+    @pl.when(is_rim)
+    def _():
+        all_sent(z_send.at[0], z_out_wide)
+        all_sent(z_send.at[1], z_out)
+        all_sent(z_send.at[2], gram_z_out)
+        gather_sent(5, gram_full)
 
     up_copies = [
         rcopy(
             result_out.at[q],
             result_in,
-            up_send.at[q],
+            up_send.at[0],
             up_recv.at[0],
             dev(layer, x, c * per + q // NC, q % NC),
         )
@@ -625,18 +707,25 @@
 
     @pl.when(is_root)
     def _():
-        root_total(1, full)
-        begin(gather(6, full, strip))
+        for span in spans:
+            root_total(1, full, span)
+            begin(gather(6, full, strip, span))
 
         @pl.when(late)
         def _():
             gram_back()
 
-        gathered(6, full, by_strip)
+        for span in spans:
+            gathered(6, full, by_strip, span)
 
         @pl.when(late)
         def _():
-            gathered(5, gram_full, by_strip)
+            gathered(5, gram_full, by_strip, narrow)
+
+
+        @pl.when(late)
+        def _():
+            gram_ref[...] = gram_full[...].reshape(gram_ref.shape)
 
         cross_gram = gram_full[pl.ds(half_blocks, half_blocks)].reshape(width, width)
         mix = dot(cross_gram, ginv_ref[...], (0, 0), HIGH)
@@ -653,8 +742,6 @@
         def _():
             upd_ref[...] = result_out[ROOT % per * NC + ROOT // per]
 
-    gram_ref[...] = gram_full[...].reshape(gram_ref.shape)
-
     @pl.when(a_other)
     def _():
         rcopy(
@@ -662,61 +749,19 @@
         ).wait_recv()
         upd_ref[...] = result_in[...]
 
-    sent(first)
-    sent(first_x)
-    sent(second)
-    sent(second_x)
-    sent(gram_core)
-    sent(gram_x)
-    sent(gram_gather)
-    sent(passes(5, gram_full, by_strip))
-
-    @pl.when(a_other)
-    def _():
-        a_remote.wait_send()
-
-    @pl.when(sends_near)
-    def _():
-        shift.wait_send()
-
-    @pl.when(sends_far)
-    def _():
-        for copy in to_relay:
-            copy.wait_send()
-
-    for q in hops:
-
-        @pl.when(relays & (y == q))
-        def _(q=q):
-            far_relay[q - 1].wait_send()
-
-    @pl.when(is_rim)
-    def _():
-        z_copy(0, z_out_wide, z_in_wide).wait_send()
-        z_copy(1, z_out, z_in).wait_send()
-        z_copy(2, gram_z_out, gram_z_in).wait_send()
-
     @pl.when(is_root)
     def _():
-        sent(bc_copies)
-        for kind, buf in ((1, full_wide), (6, full)):
-            sent(gather(kind, buf, strip))
-            sent(passes(kind, buf, by_strip))
-        for q, copy in enumerate(up_copies):
-
-            @pl.when(own_q != q)
-            def _(copy=copy):
-                copy.wait_send()
-
-    @pl.when(has_next)
-    def _():
-        sent(gather(3, pre, block))
-        sent(passes(3, pre, by_block))
-
-    @pl.when(is_root & has_prev)
-    def _():
-        for copy in pre_copies:
-            copy.wait_send()
+        all_sent(bc_send.at[0], gram_full.at[pl.ds(0, NZ - 1)])
+        gather_sent(5, gram_full)
+        gather_sent(6, full)
+
+    @pl.when(a_self)
+    def _():
+        all_sent(up_send.at[0], result_out.at[pl.ds(0, NZ - 1)])
+
+    @pl.when(is_root & a_other)
+    def _():
+        all_sent(up_send.at[0], result_out)
 
 
 def per_device(layers, layer_inputs, output_grads, input_inverse, grad_inverse):
@@ -771,25 +816,26 @@
         vmem((gram_rows, width), F32),
         vmem((NZ, gram_rows, width), F32),
         vmem((n, gram_rows, width), F32),
-        dma((7, n)),
-        dma((7, n)),
+        dma((7, 2)),
+        dma((7, 2 * NX)),
         dma((3,)),
-        dma((3, NZ)),
-        dma((1,)),
-        dma((NZ,)),
+        dma((3, 2)),
+        dma((1,)),
+        dma((2,)),
+        dma((1,)),
+        dma((1,)),
+        dma((1,)),
         dma((1,)),
         dma((1,)),
         dma((NY,)),
         dma((1,)),
-        dma((NY,)),
-        dma((NY,)),
-        dma((NZ,)),
-        dma((1,)),
-        dma((NZ,)),
-        dma((1,)),
-        dma((NZ,)),
+        dma((1,)),
+        dma((1,)),
+        dma((1,)),
+        dma((1,)),
         dma((1,)),
         dma((3,)),
+        pltpu.SemaphoreType.REGULAR,
         pltpu.SemaphoreType.REGULAR,
     ]
     whole = pl.BlockSpec(memory_space=pltpu.VMEM)

time: 74.5 us -> 71.6 us (0.961)
  Pallas kernels: 72.4 us -> 69.6 us
    pallas_call x1, Pallas kernels: 72.4 us -> 69.6 us  [per_device(): pl.pallas_call(functools.partial(kernel, layers, images, side, scale), ou...]
where the time goes in v6:
time: 71.6 us; the launch traced here: 71.5 us
  Pallas kernels  69.6 us (97%)
  local copies, waits for them, and re-layouts  1.26 us (2%)
    pallas_call x1, Pallas kernels, per_device(): pl.pallas_call(functools.partial(kernel, layers, images, side, scale), ou...  69.6 us

profile of v6, /device:TPU:25, one launch (start us, length us, event | category | flops | bytes accessed | tf_op | source)
XLA Modules:
  0.0 71.5 jit_solution(15046383457759519002)
XLA Ops:
  0.6 69.6 %kfac_step.1 = (f32[18,128]{1,0:T(8,128)S(1)}, f32[2,128,128]{2,1,0:T(8,128)S(1)}) custom-call(bf16[512,128]{1,0:T(8,128)(2,1)} %bitcast.8, bf16[512,128]{1,0:T(8,128)(2,1)} %bitcast.9, f32[18,1,1152]{2,1,0:T(1,128)} %bitcast.10, f32[128,128]{1,0:T(8,128)} %bitcast.11), custom_call_target="tpu_custom_call" | custom-call | tf_op jit(solution)/shard_map/kfac_step/pallas_call | solution.py:842
  70.2 0.6 copy.6
  70.8 0.7 copy.8

commit v7 on v6

--- a/solution.py
+++ b/solution.py
@@ -155,7 +155,7 @@
     lanes = TAPS * width
     per = NZ // NC
     own_rows = result_in.shape[0]
-    front = (TAPS + 1) // 2 * width
+    front = TAPS // 2 * width
     spans = ((0, front, 0), (front, lanes - front, 1))
     narrow = (0, width, 0)
     is_root = z == ROOT
@@ -297,6 +297,9 @@
     def _():
         a_local.start()
 
+    sizes = (NX + 2, 2 * NX, NX + 1, NX, NX + 2, NX, 2 * NX)
+    first_recv = [sum(sizes[:kind]) for kind in range(len(sizes))]
+
     def cols(view, span):
         return view.at[:, pl.ds(span[0], span[1])]
 
@@ -310,7 +313,7 @@
                 out.at[other * NX + ahead(dx)],
                 in_core.at[dx],
                 ex_send.at[kind, 0],
-                ex_recv.at[kind, dx],
+                ex_recv.at[first_recv[kind] + dx],
                 dev(layer, x, z, other),
             )
             for dx in offsets() + [0]
@@ -322,7 +325,7 @@
                 cols(out_x.at[dx], span),
                 cols(in_x.at[dx], span),
                 ex_send.at[kind, 1],
-                ex_recv.at[kind, NX + span[2]],
+                ex_recv.at[first_recv[kind] + NX + span[2]],
                 dev(layer, ahead(dx), z, c),
             )
             for dx in offsets()
@@ -344,14 +347,14 @@
         total = part[strip, :, at] + in_core[0, :, at].astype(F32)
         got = in_x.at[pl.ds(1, NX - 1), :, at]
         rcopy(
-            got, got, ex_send.at[kind, 1], ex_recv.at[kind, NX + span[2]], dev(layer, x, z, other)
+            got, got, ex_send.at[kind, 1], ex_recv.at[first_recv[kind] + NX + span[2]], dev(layer, x, z, other)
         ).wait_recv()
         for dx in range(1, NX):
             total = total + in_x[dx, :, at].astype(F32)
         return total
 
     def all_sent(sem, view):
-        rcopy(view, view, sem, ex_recv.at[0, 0], dev(layer, x, z, other)).wait_send()
+        rcopy(view, view, sem, ex_recv.at[0], dev(layer, x, z, other)).wait_send()
 
     def plane_sent(kind, in_core, in_x):
         all_sent(ex_send.at[kind, 0], in_core)
@@ -362,7 +365,7 @@
         all_sent(ex_send.at[kind, 1], buf.at[pl.ds(0, NX - 1)])
 
     def crossing(kind, out, s, got, to):
-        return rcopy(got, got, ex_send.at[kind, out], ex_recv.at[kind, s], to)
+        return rcopy(got, got, ex_send.at[kind, out], ex_recv.at[first_recv[kind] + s], to)
 
     def gather(kind, buf, own, span):
         targets = [(dx, dev(layer, ahead(dx), z, c)) for dx in offsets()]
@@ -817,7 +820,7 @@
         vmem((NZ, gram_rows, width), F32),
         vmem((n, gram_rows, width), F32),
         dma((7, 2)),
-        dma((7, 2 * NX)),
+        dma((6 * NX + 5 * NX - 3,)),
         dma((3,)),
         dma((3, 2)),
         dma((1,)),

time: 71.6 us -> 71 us (level)
  no operation moved by 1% of the time
where the time goes in v7:
time: 71 us; the launch traced here: 70.8 us
  Pallas kernels  68.9 us (97%)
  local copies, waits for them, and re-layouts  1.26 us (2%)
    pallas_call x1, Pallas kernels, per_device(): pl.pallas_call(functools.partial(kernel, layers, images, side, scale), ou...  68.9 us

profile of v7, /device:TPU:25, one launch (start us, length us, event | category | flops | bytes accessed | tf_op | source)
XLA Modules:
  0.0 70.8 jit_solution(4446067085805905241)
XLA Ops:
  0.6 68.9 %kfac_step.1 = (f32[18,128]{1,0:T(8,128)S(1)}, f32[2,128,128]{2,1,0:T(8,128)S(1)}) custom-call(bf16[512,128]{1,0:T(8,128)(2,1)} %bitcast.8, bf16[512,128]{1,0:T(8,128)(2,1)} %bitcast.9, f32[18,1,1152]{2,1,0:T(1,128)} %bitcast.10, f32[128,128]{1,0:T(8,128)} %bitcast.11), custom_call_target="tpu_custom_call" | custom-call | tf_op jit(solution)/shard_map/kfac_step/pallas_call | solution.py:845
  69.6 0.6 copy.6
  70.2 0.7 copy.8

commit v8 on v7

--- a/solution.py
+++ b/solution.py
@@ -155,7 +155,7 @@
     lanes = TAPS * width
     per = NZ // NC
     own_rows = result_in.shape[0]
-    front = TAPS // 2 * width
+    front = TAPS // 3 * width
     spans = ((0, front, 0), (front, lanes - front, 1))
     narrow = (0, width, 0)
     is_root = z == ROOT
@@ -265,7 +265,7 @@
     ]
     far_relay = [
         rcopy(
-            held(q), piece(xg_next, q), far_send.at[0], far_recv.at[q], dev(layer - q - 1, x, z, c)
+            held(q), piece(xg_next, q), far_send.at[0], far_recv.at[q - 1], dev(layer - q - 1, x, z, c)
         )
         for q in hops
     ]
@@ -830,7 +830,7 @@
         dma((1,)),
         dma((1,)),
         dma((1,)),
-        dma((NY,)),
+        dma((NY - 1,)),
         dma((1,)),
         dma((1,)),
         dma((1,)),

time: 71 us -> 71.1 us (level)
  no operation moved by 1% of the time
where the time goes in v8:
time: 71.1 us; the launch traced here: 70.9 us
  Pallas kernels  69 us (97%)
  local copies, waits for them, and re-layouts  1.26 us (2%)
    pallas_call x1, Pallas kernels, per_device(): pl.pallas_call(functools.partial(kernel, layers, images, side, scale), ou...  69 us

profile of v8, /device:TPU:25, one launch (start us, length us, event | category | flops | bytes accessed | tf_op | source)
XLA Modules:
  0.0 70.9 jit_solution(4901187332009044885)
XLA Ops:
  0.6 69.0 %kfac_step.1 = (f32[18,128]{1,0:T(8,128)S(1)}, f32[2,128,128]{2,1,0:T(8,128)S(1)}) custom-call(bf16[512,128]{1,0:T(8,128)(2,1)} %bitcast.8, bf16[512,128]{1,0:T(8,128)(2,1)} %bitcast.9, f32[18,1,1152]{2,1,0:T(1,128)} %bitcast.10, f32[128,128]{1,0:T(8,128)} %bitcast.11), custom_call_target="tpu_custom_call" | custom-call | tf_op jit(solution)/shard_map/kfac_step/pallas_call | solution.py:845
  69.7 0.6 copy.6
  70.3 0.7 copy.8
